TPU v7x, 32 devices: a whole 2x2x4 slice. The times are simulated.
32 devices in a mesh: samp: 8 (over y, x, core), cent: 4 (over z).
Axes of the slice: x: 2, y: 2, z: 4, core: 2. Of those that a mesh axis runs over, the one named last changes fastest.
Arguments:
- embeddings: float32 [16384, 1024], P(('samp', 'cent')), may hold values from -40 to 40
- assignment: int32 [16384], P(('samp', 'cent')), may hold values from 0 to 2047, as said below
- owner_map: int32 [2048], replicated, may hold values from 0 to 31, as said below
Outputs:
- centroid: float32 [2048, 1024], P(('samp', 'cent'))
- representative: float32 [2048, 1024], P(('samp', 'cent'))
- keep_weight: float32 [16384], P(('samp', 'cent'))
Inputs may be any that keep to these rules, and one draw needn't show every extreme that they name: `owner_map`: every device index, samp-major, owns exactly 64 clusters. `assignment`: of the 512 rows of one device, at most 64 lie in clusters owned by any one device; in every draw some device owns clusters that hold exactly 64 rows of every device.
All inputs are finite; a program needn't handle non-finite values.
Results may differ from a plain program's by a relative error of at most 0.0034.
Values may be sent and summed in bfloat16 or wider, within the bound.
A program may use at most 64 MiB of HBM per device.

v0:
```python
import functools

import jax
import jax.numpy as jnp
from jax import lax
from jax.experimental import pallas as pl
from jax.experimental.pallas import tpu as pltpu
from jax.sharding import PartitionSpec as P

EPSILON = 1e-06
SHARPNESS = 8.0
LANES = 128
SPILL = 65536.0
BF = jnp.bfloat16
F32 = jnp.float32
MESH = pl.DeviceIdType.MESH


def iota(shape, axis):
    return lax.broadcasted_iota(jnp.int32, shape, axis)


def row_dot(a, b):
    return lax.dot_general(a, b, (((1,), (1,)), ((), ())), preferred_element_type=F32)


def samp_half(shift):
    return (shift // 2) % 2


def pack_kernel(devices, n_cent, near, pool, emb_ref, assign_ref, owner_ref, send_ref, pool_ref, index_ref, lab_ref, meta_ref):
    rows = emb_ref.shape[0]
    clusters = owner_ref.shape[1]
    upper = (iota((rows, rows), 0) < iota((rows, rows), 1)).astype(BF)
    owner = owner_ref[...]
    owner_hot = (iota((devices, clusters), 0) == owner).astype(F32)
    base = jnp.zeros((devices, 1), F32)
    ranks = []
    for start in range(0, clusters, rows):
        part = owner_hot[:, start:start + rows]
        before = jnp.dot(part.astype(BF), upper, preferred_element_type=F32) + base
        ranks.append(jnp.sum(part * before, axis=0, keepdims=True))
        base = base + jnp.sum(part, axis=1, keepdims=True)
    rank = jnp.concatenate(ranks, axis=1)
    assign = assign_ref[...]
    pick = (iota((clusters, rows), 0) == assign).astype(BF)
    which = iota((8, clusters), 0)
    table = jnp.where(which == 0, owner.astype(F32), jnp.where(which == 1, rank, 0.0)).astype(BF)
    found = jnp.dot(table, pick, preferred_element_type=F32)
    dest = found[0:1, :].astype(jnp.int32)
    label = found[1:2, :] + 1.0
    dest_hot = (iota((devices, rows), 0) == dest).astype(F32)
    before = jnp.dot(dest_hot.astype(BF), upper, preferred_element_type=F32)
    within = jnp.sum(dest_hot * before, axis=0, keepdims=True)
    over = (within >= near).astype(F32)
    over_before = jnp.dot(
        jnp.broadcast_to(over, (8, rows)).astype(BF), upper, preferred_element_type=F32
    )[0:1, :]
    excess = jnp.sum(over, axis=1, keepdims=True) > pool
    within = within.astype(jnp.int32)
    is_over = over > 0.0
    pool_at = over_before.astype(jnp.int32)
    samp = lax.axis_index("samp")
    cent = lax.axis_index("cent")
    n_samp = devices // n_cent
    span = n_samp * near
    shift = (dest // n_cent + n_samp - samp) % n_samp
    toward = dest % n_cent
    near_lane = shift * near + within
    pair_lane = (samp_half(shift) * n_cent + cent) * pool + jnp.minimum(pool_at, pool - 1)
    column = jnp.where(is_over, span + pair_lane, near_lane)
    col_hot = (iota((lab_ref.shape[2], rows), 0) == column).astype(BF)
    labels = row_dot((dest_hot * label).astype(BF), col_hot)
    lane_hot = (iota((n_cent, rows), 0) == jnp.where(is_over, -1, toward)).astype(F32)
    lane_before = jnp.dot(lane_hot.astype(BF), upper, preferred_element_type=F32)
    packed = jnp.sum(lane_hot * lane_before, axis=0, keepdims=True).astype(jnp.int32)
    limit = send_ref.shape[1]
    crowded = jnp.sum(
        jnp.where((packed >= limit) & jnp.logical_not(is_over), 1.0, 0.0), axis=1, keepdims=True
    ) > 0.0
    lab_ref[:, 0, :] = labels + jnp.where(excess | crowded, SPILL, 0.0)
    seat_hot = (iota((index_ref.shape[2], rows), 0) == packed).astype(BF)
    index_ref[:, 0, :] = row_dot((lane_hot * (near_lane + 1).astype(F32)).astype(BF), seat_hot)
    meta_ref[...] = jnp.where(iota((8, rows), 0) == 0, dest, column)
    emb = emb_ref[...]
    unit = (emb * lax.rsqrt(jnp.sum(emb * emb, axis=1, keepdims=True) + EPSILON)).astype(BF)
    seat = jnp.where(is_over, -1, jnp.where(packed < limit, toward * limit + packed, -1))
    for c in range(n_cent):
        hot = (iota((limit, rows), 0) + c * limit == seat).astype(BF)
        send_ref[c] = jnp.dot(hot, unit, preferred_element_type=F32).astype(BF)
    pool_hot = (iota((pool, rows), 0) == jnp.where(is_over, pool_at, -1)).astype(BF)
    pool_ref[...] = jnp.dot(pool_hot, unit, preferred_element_type=F32).astype(BF)


def who(n_cent, index):
    return (index // n_cent, index % n_cent)


def enter(n_samp, n_cent, me):
    devices = n_samp * n_cent
    barrier = pltpu.get_barrier_semaphore()

    def greet(k, _):
        pl.semaphore_signal(
            barrier, inc=1, device_id=who(n_cent, (me + k) % devices), device_id_type=MESH
        )
        return 0

    lax.fori_loop(1, devices, greet, 0)
    pl.semaphore_wait(barrier, devices - 1)


def dedup_kernel(
    n_samp, n_cent, send_ref, pool_ref, index_ref, lab_ref, cent_ref, rep_ref, back_ref, tags_ref,
    lane_ref, seat_ref, stage_ref, near_ref, pools_ref, labs_ref, x_ref, col_ref, turn_ref, dens_ref,
    sums_ref, out_ref,
    own_sem, row_out, row_in, lab_out, lab_in, near_out, near_in, far_out, far_in, back_out, back_in,
    lane_out, lane_in, seat_out, seat_in, fwd_out,
):
    samp = lax.axis_index("samp")
    cent = lax.axis_index("cent")
    me = samp * n_cent + cent
    per_owner = cent_ref.shape[0]
    near = near_ref.shape[2]
    pool = pools_ref.shape[2]
    width = x_ref.shape[1]
    limit = lane_ref.shape[1]
    span = n_samp * near
    block = span
    quads = n_samp // 2
    count = n_cent + quads
    evens = list(range(0, n_samp, 2))

    def loop(low, high, body):
        def step(k, _):
            body(k)
            return 0
        lax.fori_loop(low, high, step, 0)

    def target(shift, c):
        return ((samp + shift) % n_samp, c)

    def near_copy(c, slot):
        return pltpu.make_async_remote_copy(
            pool_ref, pools_ref.at[0, slot], near_out.at[c], near_in.at[slot],
            device_id=(samp, c), device_id_type=MESH,
        )

    def lane_copy(c, slot):
        return pltpu.make_async_remote_copy(
            send_ref.at[c], lane_ref.at[slot], lane_out.at[c], lane_in.at[slot],
            device_id=(samp, c), device_id_type=MESH,
        )

    def seat_copy(c, slot):
        return pltpu.make_async_remote_copy(
            index_ref.at[c], seat_ref.at[slot], seat_out.at[c], seat_in.at[slot],
            device_id=(samp, c), device_id_type=MESH,
        )

    def row_copy(k, c):
        return pltpu.make_async_remote_copy(
            stage_ref.at[c, k], near_ref.at[c, k], row_out.at[k, c], row_in.at[k, c],
            device_id=target(k, cent), device_id_type=MESH,
        )

    def lab_copy(k, c, slot):
        s, t = target(k, c)
        return pltpu.make_async_remote_copy(
            lab_ref.at[s * n_cent + t], labs_ref.at[k, slot], lab_out.at[k, c], lab_in.at[k, slot],
            device_id=(s, t), device_id_type=MESH,
        )

    def far_copy(k):
        return pltpu.make_async_remote_copy(
            pools_ref.at[0], pools_ref.at[k], far_out.at[k], far_in.at[k],
            device_id=target(k, cent), device_id_type=MESH,
        )

    turn_by = 1 + (n_samp - 2) * (samp % 2)

    def forward(k):
        slot = (k + turn_by) % n_samp
        return pltpu.make_async_remote_copy(
            pools_ref.at[k], pools_ref.at[slot], fwd_out.at[k], far_in.at[slot],
            device_id=target(turn_by, cent), device_id_type=MESH,
        )

    def back_copy(k, c, slot, at_c):
        s = (samp + n_samp - k) % n_samp
        return pltpu.make_async_remote_copy(
            out_ref.at[c, samp_pair(k)], back_ref.at[slot], back_out.at[k, c], back_in.at[k, at_c],
            device_id=(s, c), device_id_type=MESH,
        )

    def samp_pair(k):
        return (k // 4) + (k % 2) * (n_samp // 4)

    def others(k, body):
        loop(1 if k == 0 else 0, n_cent, lambda c: body((cent + c) % n_cent))

    own = [
        pltpu.make_async_copy(send_ref.at[cent], lane_ref.at[cent], own_sem.at[0]),
        pltpu.make_async_copy(lab_ref.at[me], labs_ref.at[0, cent], own_sem.at[1]),
        pltpu.make_async_copy(pool_ref, pools_ref.at[0, cent], own_sem.at[2]),
        pltpu.make_async_copy(index_ref.at[cent], seat_ref.at[cent], own_sem.at[3]),
    ]
    for copy in own:
        copy.start()
    enter(n_samp, n_cent, me)
    others(0, lambda c: seat_copy(c, cent).start())
    others(0, lambda c: near_copy(c, cent).start())
    others(0, lambda c: lane_copy(c, cent).start())
    for k in range(n_samp):
        others(k, lambda c: lab_copy(k, c, cent).start())
    turn_ref[...] = jnp.zeros_like(turn_ref)
    sums_ref[...] = jnp.zeros_like(sums_ref)
    for copy in own:
        copy.wait()

    def spread(c):
        seat = seat_ref[c][:, 0:limit].astype(jnp.int32)
        hot = (iota((span, limit), 0) + 1 == seat).astype(BF)
        rows = jnp.dot(hot, lane_ref[c], preferred_element_type=F32).astype(BF)
        stage_ref[c] = rows.reshape(n_samp, near, width)

    def pass_on(c):
        loop(1, n_samp, lambda k: row_copy(k, c).start())

    spread(cent)
    others(0, lambda c: near_copy(c, c).wait_recv())
    pass_on(cent)
    for k in evens[1:]:
        far_copy(k).start()
    forward(0).start()
    for k in range(n_samp):
        others(k, lambda c: lab_copy(k, c, c).wait_recv())

    def score(p, load, tag):
        at = p * block
        load(at)
        tags_ref[p] = tag
        for start in range(0, block, LANES):
            chunk = jnp.broadcast_to(tag[:, start:start + LANES], (LANES, LANES))
            col_ref[at + start:at + start + LANES, :] = jnp.transpose(chunk)
        fresh = x_ref[at:at + block, :]
        member = (tag == (iota((per_owner, block), 0) + 1).astype(F32)).astype(BF)
        sums_ref[...] += jnp.dot(member, fresh, preferred_element_type=F32)

        def piece(top, height):
            gram = row_dot(x_ref[pl.ds(top, height), :], fresh)
            left = col_ref[pl.ds(top, height), :]
            same = jnp.concatenate([left] * (block // LANES), axis=1) == tag
            return jnp.where(same, jnp.exp(SHARPNESS * (gram - 1.0)), 0.0)

        def both(top, height):
            part = piece(top, height)
            folded = part[:, 0:LANES]
            for start in range(LANES, block, LANES):
                folded = folded + part[:, start:start + LANES]
            turn_ref[pl.ds(top, height), :] += folded
            return jnp.sum(part, axis=0, keepdims=True)

        total = jnp.sum(piece(at, block), axis=0, keepdims=True)
        if p >= 2:
            total = lax.fori_loop(
                0, p // 2,
                lambda j, t: t + both(pl.multiple_of(j * 2 * block, 2 * block), 2 * block),
                total,
            )
        if p % 2:
            total = total + both((p - 1) * block, block)
        dens_ref[p] = total

    def near_block(p, i):
        c = (cent + i) % n_cent
        tag = labs_ref[0, c][:, 0:span]
        for k in range(1, n_samp):
            tag = tag + labs_ref[k, c][:, 0:span]
        loop(1, n_samp, lambda k: row_copy(k, c).wait_recv())

        def load(at):
            x_ref[at:at + near, :] = stage_ref[c, 0]
            x_ref[at + near:at + block, :] = near_ref[c, 1:].reshape(block - near, width)

        score(p, load, tag)

    def pool_block(p, q):
        first = 4 * (q % (n_samp // 4)) + q // (n_samp // 4)
        half = n_cent * pool
        tag = jnp.zeros((1, block), F32)
        for k in (first, first + 2):
            for c in range(n_cent):
                tag = tag + labs_ref[k, c][:, span:span + block]
            if k > 0:
                far_copy(k).wait_recv()
                if k % 2 == 0:
                    forward(k).start()

        def load(at):
            x_ref[at:at + half, :] = pools_ref[first].reshape(half, width)
            x_ref[at + half:at + block, :] = pools_ref[first + 2].reshape(half, width)

        score(p, load, tag)

    order = []

    def run(is_near, which):
        order.append((is_near, which))
        if is_near:
            near_block(len(order) - 1, which)
        else:
            pool_block(len(order) - 1, which)

    for i in range(1, n_cent):
        c = (cent + i) % n_cent
        seat_copy(c, c).wait_recv()
        lane_copy(c, c).wait_recv()
        spread(c)
        pass_on(c)
        if i == 1:
            run(True, 0)
        for q in range((i - 1) * quads // (n_cent - 1), i * quads // (n_cent - 1)):
            run(False, q)
    for i in range(1, n_cent):
        run(True, i)

    sums = sums_ref[...]
    scale = lax.rsqrt(jnp.sum(sums * sums, axis=1, keepdims=True) + EPSILON)
    centroid = sums * scale
    cent_ref[...] = centroid
    high = centroid.astype(BF)
    low = (centroid - high.astype(F32)).astype(BF)
    pair = jnp.concatenate([high, low], axis=0)
    for p in range(count):
        at = p * block
        tag = tags_ref[p]
        valid = tag > 0.0
        member = tag == (iota((per_owner, block), 0) + 1).astype(F32)
        towards = row_dot(pair, x_ref[at:at + block, :])
        towards = towards[0:per_owner, :] + towards[per_owner:, :]
        similar = jnp.sum(jnp.where(member, towards, 0.0), axis=0, keepdims=True)
        flipped = []
        for start in range(at, at + block, LANES):
            flipped.append(
                jnp.sum(jnp.transpose(turn_ref[start:start + LANES, :]), axis=0, keepdims=True)
            )
        density = jnp.where(valid, dens_ref[p] + jnp.concatenate(flipped, axis=1), 1.0)
        weight = jnp.where(valid, jnp.exp(1.0 - similar) / density, 0.0)
        dens_ref[p] = weight
        is_near, which = order[p]
        if is_near:
            c = (cent + which) % n_cent
            for q in range(quads):
                out_ref[c, q, :, 0:span] = weight
        else:
            for c in range(n_cent):
                out_ref[c, which, :, span:span + block] = weight
    mine = pltpu.make_async_copy(out_ref.at[cent, 0], back_ref.at[me], own_sem.at[4])
    mine.start()
    mine.wait()
    for k in range(n_samp):
        others(k, lambda c: back_copy(k, c, me, cent).start())
    mixed = jnp.zeros(sums_ref.shape, F32)
    for p in range(count):
        member = tags_ref[p] == (iota((per_owner, block), 0) + 1).astype(F32)
        mixed = mixed + jnp.dot(
            jnp.where(member, dens_ref[p], 0.0).astype(BF), x_ref[p * block:(p + 1) * block, :],
            preferred_element_type=F32,
        )
    rep_ref[...] = mixed * lax.rsqrt(jnp.sum(mixed * mixed, axis=1, keepdims=True) + EPSILON)
    others(0, lambda c: seat_copy(c, cent).wait_send())
    others(0, lambda c: near_copy(c, cent).wait_send())
    others(0, lambda c: lane_copy(c, cent).wait_send())
    loop(0, n_cent, lambda c: loop(1, n_samp, lambda k: row_copy(k, c).wait_send()))
    for k in range(n_samp):
        others(k, lambda c: lab_copy(k, c, cent).wait_send())
        if k % 2 == 0:
            forward(k).wait_send()
            if k > 0:
                far_copy(k).wait_send()
        others(k, lambda c: back_copy(k, c, me, cent).wait_send())
    for k in range(n_samp):
        others(k, lambda c: back_copy(k, c, ((samp + k) % n_samp) * n_cent + c, c).wait_recv())


def pick_kernel(back_ref, meta_ref, tags_ref, keep_ref, top_ref):
    top_ref[0, 0] = jnp.max(tags_ref[:, 0, :])
    devices = back_ref.shape[0]
    rows = meta_ref.shape[1]
    meta = meta_ref[...]
    dest_hot = (iota((devices, rows), 0) == meta[0:1, :]).astype(F32)
    spread = lax.dot_general(
        back_ref[:, 0, :], dest_hot, (((0,), (0,)), ((), ())),
        preferred_element_type=F32, precision=lax.Precision.HIGHEST,
    )
    hit = iota((back_ref.shape[2], rows), 0) == meta[1:2, :]
    keep_ref[...] = jnp.sum(jnp.where(hit, spread, 0.0), axis=0, keepdims=True)


def all_pairs(arrived, arrived_tags, validity, block_size):
    slot_count, feature_width = arrived.shape
    block_count = slot_count // block_size

    def score_block(pieces):
        block_rows, block_tags = pieces
        gram = jnp.einsum("rd,qd->rq", block_rows, arrived, preferred_element_type=jnp.float32)
        same_cluster = (block_tags[:, None] == arrived_tags[None, :]) & validity[None, :]
        similar = jnp.sum(jnp.where(same_cluster, gram, 0.0), axis=1)
        density = jnp.sum(jnp.where(same_cluster, jnp.exp(SHARPNESS * (gram - 1.0)), 0.0), axis=1)
        return (similar, density)

    similar, density = lax.map(
        score_block,
        (
            arrived.reshape(block_count, block_size, feature_width),
            arrived_tags.reshape(block_count, block_size),
        ),
    )
    return (similar.reshape(slot_count), density.reshape(slot_count))


def full_capacity(embeddings, assignment, owner_map):
    row_count, feature_width = embeddings.shape
    devices = lax.axis_size("samp") * lax.axis_size("cent")
    clusters = owner_map.shape[0]
    per_owner = clusters // devices
    capacity = 4 * row_count // devices
    slot_count = devices * capacity
    unit_rows = (
        embeddings * lax.rsqrt(jnp.sum(embeddings * embeddings, axis=1, keepdims=True) + EPSILON)
    ).astype(jnp.bfloat16)
    destination = owner_map[assignment]
    cluster_order = jnp.argsort(owner_map, stable=True)
    position = (
        jnp.zeros((clusters,), jnp.int32)
        .at[cluster_order]
        .set(jnp.arange(clusters, dtype=jnp.int32))
    )
    local_rank = position[assignment] - destination * per_owner
    dest_onehot = (destination[:, None] == jnp.arange(devices, dtype=jnp.int32)[None, :]).astype(
        jnp.int32
    )
    within_rank = jnp.sum(jnp.cumsum(dest_onehot, axis=0) * dest_onehot, axis=1) - 1
    slot_index = destination * capacity + within_rank
    outgoing = jnp.zeros((slot_count, feature_width), jnp.bfloat16).at[slot_index].set(unit_rows)
    labels = (
        jnp.zeros((slot_count,), jnp.bfloat16)
        .at[slot_index]
        .set((local_rank + 1).astype(jnp.bfloat16))
    )
    arrived, arrived_labels = (
        lax.all_to_all(outgoing, ("samp", "cent"), split_axis=0, concat_axis=0, tiled=True),
        lax.all_to_all(labels, ("samp", "cent"), split_axis=0, concat_axis=0, tiled=True),
    )
    arrived_tags = arrived_labels.astype(jnp.int32) - 1
    validity = arrived_tags >= 0
    block_size = min(512, slot_count)
    similar, density = all_pairs(arrived, arrived_tags, validity, block_size)
    member = arrived_tags[None, :] == jnp.arange(per_owner, dtype=jnp.int32)[:, None]
    member_bf = member.astype(jnp.bfloat16)
    cluster_sums = jnp.dot(member_bf, arrived, preferred_element_type=jnp.float32)
    inverse_norm = lax.rsqrt(jnp.sum(cluster_sums * cluster_sums, axis=1) + EPSILON)
    row_scale = jnp.sum(member.astype(jnp.float32) * inverse_norm[:, None], axis=0)
    spread = 1.0 - similar * row_scale
    weight = jnp.where(validity, jnp.exp(spread) / jnp.where(validity, density, 1.0), 0.0)
    weighted = jnp.dot(
        member_bf * weight.astype(jnp.bfloat16)[None, :],
        arrived,
        preferred_element_type=jnp.float32,
    )
    centroid = cluster_sums * inverse_norm[:, None]
    representative = weighted * lax.rsqrt(
        jnp.sum(weighted * weighted, axis=1, keepdims=True) + EPSILON
    )
    returned = lax.all_to_all(weight, ("samp", "cent"), split_axis=0, concat_axis=0, tiled=True)
    keep_weight = returned[slot_index]
    return (centroid, representative, keep_weight)


def on_device(embeddings, assignment, owner_map):
    rows, width = embeddings.shape
    n_samp = lax.axis_size("samp")
    n_cent = lax.axis_size("cent")
    devices = n_samp * n_cent
    clusters = owner_map.shape[0]
    per_owner = clusters // devices
    capacity = 4 * rows // devices
    near = capacity // 2
    pool = capacity - near
    vmem = pl.BlockSpec(memory_space=pltpu.VMEM)
    anywhere = pl.BlockSpec(memory_space=pl.ANY)
    shape = jax.ShapeDtypeStruct
    dma = pltpu.SemaphoreType.DMA
    block = n_samp * near
    blocks = n_cent + n_samp // 2
    slots = blocks * block
    limit = 21 * block // 32 // 8 * 8
    room = (limit + LANES - 1) // LANES * LANES
    send, pooled, index, labels, meta = pl.pallas_call(
        functools.partial(pack_kernel, devices, n_cent, near, pool),
        out_shape=(
            shape((n_cent, limit, width), BF),
            shape((pool, width), BF),
            shape((n_cent, 1, room), F32),
            shape((devices, 1, 2 * block), F32),
            shape((8, rows), jnp.int32),
        ),
        in_specs=[vmem] * 3,
        out_specs=(vmem,) * 5,
        name="pack",
    )(embeddings, assignment.reshape(1, rows), owner_map.reshape(1, clusters))
    centroid, representative, back, tags = pl.pallas_call(
        functools.partial(dedup_kernel, n_samp, n_cent),
        out_shape=(
            shape((per_owner, width), F32),
            shape((per_owner, width), F32),
            shape((devices, 1, 2 * block), F32),
            shape((blocks, 1, block), F32),
        ),
        in_specs=[anywhere] * 4,
        out_specs=(vmem,) * 4,
        scratch_shapes=[
            pltpu.VMEM((n_cent, limit, width), BF),
            pltpu.VMEM((n_cent, 1, room), F32),
            pltpu.VMEM((n_cent, n_samp, near, width), BF),
            pltpu.VMEM((n_cent, n_samp, near, width), BF),
            pltpu.VMEM((n_samp, n_cent, pool, width), BF),
            pltpu.VMEM((n_samp, n_cent, 1, 2 * block), F32),
            pltpu.VMEM((slots, width), BF),
            pltpu.VMEM((slots, LANES), F32),
            pltpu.VMEM((slots, LANES), F32),
            pltpu.VMEM((blocks, 1, block), F32),
            pltpu.VMEM((per_owner, width), F32),
            pltpu.VMEM((n_cent, n_samp // 2, 1, 2 * block), F32),
            dma((5,)),
            dma((n_samp, n_cent)), dma((n_samp, n_cent)), dma((n_samp, n_cent)), dma((n_samp, n_cent)),
            dma((n_cent,)), dma((n_cent,)), dma((n_samp,)), dma((n_samp,)),
            dma((n_samp, n_cent)), dma((n_samp, n_cent)),
            dma((n_cent,)), dma((n_cent,)), dma((n_cent,)), dma((n_cent,)), dma((n_samp,)),
        ],
        compiler_params=pltpu.CompilerParams(collective_id=0, has_side_effects=True),
        name="dedup",
    )(send, pooled, index, labels)
    keep, top = pl.pallas_call(
        pick_kernel,
        out_shape=(shape((1, rows), F32), shape((1, 1), F32)),
        in_specs=[vmem] * 3,
        out_specs=(vmem, pl.BlockSpec(memory_space=pltpu.SMEM)),
        name="pick",
    )(back, meta, tags)
    keep = keep.reshape(rows)

    def fast(embeddings, assignment, owner_map, centroid, representative, keep):
        return centroid, representative, keep

    def slow(embeddings, assignment, owner_map, centroid, representative, keep):
        return full_capacity(embeddings, assignment, owner_map)

    spilled = top[0, 0] >= SPILL
    return lax.cond(
        spilled, slow, fast, embeddings, assignment, owner_map, centroid, representative, keep
    )


def solution(mesh):
    in_specs = (P(("samp", "cent"), None), P(("samp", "cent")), P())
    out_specs = (P(("samp", "cent"), None), P(("samp", "cent"), None), P(("samp", "cent")))
    return jax.shard_map(
        on_device, mesh=mesh, in_specs=in_specs, out_specs=out_specs, check_vma=False
    )
```

profile of v0, /device:TPU:0, one launch (start us, length us, event | category | flops | bytes accessed | tf_op | source)
XLA Modules:
  0.0 87.6 jit_solution(14064151894602112946)
XLA Ops:
  0.6 5.0 %pack.1 = (bf16[4,168,1024]{2,1,0:T(8,128)(2,1)}, bf16[32,1024]{1,0:T(8,128)(2,1)}, f32[4,1,256]{2,1,0:T(1,128)}, f32[32,1,512]{2,1,0:T(1,128)}, s32[8,512]{1,0:T(8,128)}) custom-call(f32[512,1024]{1,0:T(8,128)} %emb_ref.1, s32[1,512]{1,0:T(1,128)} %bitcast.63, s32[1,2048]{1,0:T(1,128)} %bitcast.52), custom_call_target="tpu_custom_call" | custom-call | tf_op jit(solution)/shard_map/pack/pallas_call | solution.py:500
  5.6 77.3 %dedup.1 = (f32[64,1024]{1,0:T(8,128)S(1)}, f32[64,1024]{1,0:T(8,128)S(1)}, f32[32,1,512]{2,1,0:T(1,128)}, f32[8,1,256]{2,1,0:T(1,128)}) custom-call(bf16[4,168,1024]{2,1,0:T(8,128)(2,1)} %get-tuple-element.139.send_ref, bf16[32,1024]{1,0:T(8,128)(2,1)} %get-tuple-element.140.pool_ref, f32[4,1,256]{2,1,0:T(1,128)} %get-tuple-element.141.index_ref, ...), custom_call_target="tpu_custom_call" | custom-call | tf_op jit(solution)/shard_map/dedup/pallas_call | solution.py:513
  82.9 2.4 %pick.1 = (f32[1,512]{1,0:T(1,128)S(1)}, f32[1,1]{1,0:T(1,128)}) custom-call(f32[32,1,512]{2,1,0:T(1,128)} %get-tuple-element.143.back_ref, s32[8,512]{1,0:T(8,128)} %get-tuple-element.144.meta_ref, f32[8,1,256]{2,1,0:T(1,128)} %get-tuple-element.145.tags_ref), custom_call_target="tpu_custom_call" | custom-call | tf_op jit(solution)/shard_map/pick/pallas_call | solution.py:545
  85.9 0.2 conditional.1
  86.2 0.0 copy-start.1
  86.2 0.7 copy.38
  86.9 0.7 copy.39
  87.6 0.0 copy-done.1
Async XLA Ops:
  86.2 1.4 %copy-start.1 = (f32[512]{0:T(512)}, f32[512]{0:T(512)S(1)}, u32[]{:S(2)}) copy-start(f32[512]{0:T(512)S(1)} %get-tuple-element.276) | copy-start | bytes 6148
where the time goes:
time: 87.8 us; the launch traced here: 87.6 us
  Pallas kernels  84.6 us (96%)
  local copies, waits for them, and re-layouts  1.41 us (2%)
  between operations  1.31 us (1%)
    pallas_call x1, Pallas kernels, on_device(): pl.pallas_call(functools.partial(dedup_kernel, n_samp, n_cent), out_shape...  77.3 us
    pallas_call x1, Pallas kernels, on_device(): pl.pallas_call(functools.partial(pack_kernel, devices, n_cent, near, pool...  5.01 us
    pallas_call x1, Pallas kernels, on_device(): pl.pallas_call(pick_kernel, out_shape=(shape((1, rows), F32), shape((1, 1...  2.36 us

commit v1 on v0

v1 whole, which is shorter than its diff:
```python
import functools

import jax
import jax.numpy as jnp
from jax import lax
from jax.experimental import pallas as pl
from jax.experimental.pallas import tpu as pltpu
from jax.sharding import PartitionSpec as P

EPSILON = 1e-06
SHARPNESS = 8.0
LANES = 128
HALF = LANES // 2
SPILL = 65536.0
BF = jnp.bfloat16
F32 = jnp.float32
I32 = jnp.int32
MESH = pl.DeviceIdType.MESH


def iota(shape, axis):
    return lax.broadcasted_iota(jnp.int32, shape, axis)


def row_dot(a, b):
    return lax.dot_general(a, b, (((1,), (1,)), ((), ())), preferred_element_type=F32)


def dot(a, b):
    return jnp.dot(a, b, preferred_element_type=F32)


def column_sum(a):
    return jnp.sum(a, axis=0, keepdims=True)


def loop(low, high, body):
    def step(k, _):
        body(k)
        return 0

    lax.fori_loop(low, high, step, 0)


def flip(index, bits, size):
    if size & (size - 1):
        return (index + bits) % size
    step = 1
    out = index
    while step <= bits:
        if bits & step:
            out = out + step * (1 - 2 * ((index // step) % 2))
        step *= 2
    return out


def dedup_kernel(
    n_samp, n_cent, groups, per_owner, quota, bin_rows, lane_rows,
    emb_hbm, assign_ref, owner_ref, cent_ref, rep_ref, back_ref, meta_ref,
    emb_ref, upper_ref, direct_ref, x_ref, tag_out_ref, tag_ref, bin_out_ref, bin_ref, note_out_ref, note_ref,
    lane_out_ref, lane_ref, mark_out_ref, mark_ref, col_ref, turn_ref, cent_out_ref, rep_out_ref, weight_ref,
    load_sem, own_sem, direct_out, direct_in, tag_out, tag_in, bin_out, bin_in, note_out, note_in,
    lane_out, lane_in, mark_out, mark_in, cent_send, cent_recv, rep_send, rep_recv, weight_out, weight_in,
):
    samp = lax.axis_index("samp")
    cent = lax.axis_index("cent")
    me = samp * n_cent + cent
    devices = n_samp * n_cent
    rows, width = emb_ref.shape
    table_rows = owner_ref.shape[0]
    span = devices // groups
    near = n_cent // groups
    each = per_owner // span
    wide = each * (width // LANES)
    group = cent // near
    mine = samp * near + cent % near
    slots = devices * quota
    late_slots = n_cent * HALF
    held = n_samp * HALF

    def who(index):
        return (index // n_cent, index % n_cent)

    def member(index):
        return (index // near, group * near + index % near)

    def remote(source, target, sent, received, device):
        return pltpu.make_async_remote_copy(
            source, target, sent, received, device_id=device, device_id_type=MESH
        )

    part = rows // load_sem.shape[0]
    loads = [
        pltpu.make_async_copy(
            emb_hbm.at[pl.ds(i * part, part)], emb_ref.at[pl.ds(i * part, part)], load_sem.at[i]
        )
        for i in range(load_sem.shape[0])
    ]
    for copy in loads:
        copy.start()
    barrier = pltpu.get_barrier_semaphore()
    loop(
        1, devices,
        lambda k: pl.semaphore_signal(
            barrier, inc=1, device_id=who((me + k) % devices), device_id_type=MESH
        ),
    )

    bin_ref[:, bin_rows:, :] = jnp.zeros((n_samp, HALF - bin_rows, width), BF)
    lane_ref[:, lane_rows:, :] = jnp.zeros((n_cent, HALF - lane_rows, width), BF)
    upper_ref[...] = (iota(upper_ref.shape, 0) < iota(upper_ref.shape, 1)).astype(BF)

    owner = owner_ref[...]
    owner_hot = (iota((table_rows, devices, LANES), 1) == owner[:, None, :]).astype(F32)
    before = dot(
        owner_hot.reshape(table_rows * devices, LANES).astype(BF), upper_ref[0:LANES, 0:LANES]
    ).reshape(table_rows, devices, LANES)
    base = jnp.zeros((devices, 1), F32)
    ranks = []
    for i in range(table_rows):
        ranks.append(column_sum(owner_hot[i] * (before[i] + base)))
        base = base + jnp.sum(owner_hot[i], axis=1, keepdims=True)
    table = jnp.concatenate([owner.astype(F32)] + ranks, axis=0).astype(BF)
    assign = assign_ref[...]
    found = dot(table, (iota((LANES, rows), 0) == assign % LANES).astype(BF))
    line = iota((table_rows, rows), 0) == assign // LANES
    own = column_sum(jnp.where(line, found[0:table_rows, :], 0.0)).astype(I32)
    rank = column_sum(jnp.where(line, found[table_rows:, :], 0.0)).astype(I32)
    is_high = rank >= per_owner // 2
    fold = jnp.where(is_high, per_owner - 1 - rank, rank)
    place = fold % span
    own_cent = own % n_cent
    to_samp = place // near
    to_cent = (own_cent // near) * near + place % near
    chosen = fold // span + jnp.where(is_high, each // 2, 0)
    tag = (((own // n_cent) * near + own_cent % near) * each + chosen + 1).astype(F32)
    dest = to_samp * n_cent + to_cent

    upper = upper_ref[0:rows, 0:rows]
    dest_hot = (iota((devices, rows), 0) == dest).astype(F32)
    within = column_sum(dest_hot * dot(dest_hot.astype(BF), upper)).astype(I32)
    is_late = within >= quota
    late_hot = ((iota((n_samp, rows), 0) == to_samp) & is_late).astype(F32)
    place = column_sum(late_hot * dot(late_hot.astype(BF), upper)).astype(I32)
    crowded = jnp.max(jnp.where(is_late & (place >= bin_rows), 1.0, 0.0), axis=1, keepdims=True)
    meta_ref[...] = jnp.where(
        iota((8, rows), 0) == 0, dest, jnp.where(is_late, HALF + place, within)
    )

    pack = LANES // quota
    seat = jnp.where(is_late, -1, (me % pack) * quota + within)
    tag_out_ref[:, 0, :] = row_dot(
        (dest_hot * tag).astype(BF), (iota((LANES, rows), 0) == seat).astype(BF)
    )
    seat = jnp.where(is_late & (place < bin_rows), (samp % 2) * HALF + place, -1)
    notes = row_dot(
        jnp.concatenate([late_hot * tag, late_hot * to_cent.astype(F32)], axis=0).astype(BF),
        (iota((LANES, rows), 0) == seat).astype(BF),
    )
    note_out_ref[:, 0, :] = notes[0:n_samp, :] + LANES * notes[n_samp:, :]

    for copy in loads:
        copy.wait()
    emb = emb_ref[...]
    unit = (emb * lax.rsqrt(jnp.sum(emb * emb, axis=1, keepdims=True) + EPSILON)).astype(BF)
    seat = jnp.where(is_late & (place < bin_rows), to_samp * bin_rows + place, -1)
    hot = (iota((n_samp * bin_rows, rows), 0) == seat).astype(BF)
    bin_out_ref[...] = dot(hot, unit).astype(BF).reshape(n_samp, bin_rows, width)
    seat = jnp.where(is_late, -1, dest * quota + within)
    for start in range(0, slots, 2 * LANES):
        hot = (iota((2 * LANES, rows), 0) + start == seat).astype(BF)
        direct_ref[start // quota:(start + 2 * LANES) // quota] = (
            dot(hot, unit).astype(BF).reshape(2 * LANES // quota, quota, width)
        )

    def bin_copy(to, slot):
        return remote(
            bin_out_ref.at[to], bin_ref.at[slot, pl.ds(0, bin_rows)], bin_out.at[to], bin_in.at[slot], (to, cent)
        )

    def note_copy(to, slot):
        return remote(note_out_ref.at[to], note_ref.at[slot], note_out.at[to], note_in.at[slot], (to, cent))

    def direct_copy(to, slot):
        return remote(direct_ref.at[to], x_ref.at[slot], direct_out.at[to], direct_in.at[slot], who(to))

    def tag_copy(to, slot):
        return remote(tag_out_ref.at[to], tag_ref.at[slot], tag_out.at[to], tag_in.at[slot], who(to))

    def lane_copy(to, slot):
        return remote(
            lane_out_ref.at[to, pl.ds(0, lane_rows)], lane_ref.at[slot, pl.ds(0, lane_rows)],
            lane_out.at[to], lane_in.at[slot], (samp, to),
        )

    def mark_copy(to, slot):
        return remote(mark_out_ref.at[to], mark_ref.at[slot], mark_out.at[to], mark_in.at[slot], (samp, to))

    def cent_copy(to, slot):
        return remote(cent_out_ref.at[to], cent_ref.at[slot], cent_send.at[to], cent_recv.at[slot], member(to))

    def rep_copy(to, slot):
        return remote(rep_out_ref.at[to], rep_ref.at[slot], rep_send.at[to], rep_recv.at[slot], member(to))

    def weight_copy(to, slot):
        return remote(weight_ref.at[to], back_ref.at[slot], weight_out.at[to], weight_in.at[slot], who(to))

    def peers(count, index, body):
        loop(1, count, lambda k: body((index + k) % count))

    local = [
        pltpu.make_async_copy(bin_out_ref.at[samp], bin_ref.at[samp, pl.ds(0, bin_rows)], own_sem.at[0]),
        pltpu.make_async_copy(note_out_ref.at[samp], note_ref.at[samp], own_sem.at[1]),
        pltpu.make_async_copy(direct_ref.at[me], x_ref.at[me], own_sem.at[2]),
        pltpu.make_async_copy(tag_out_ref.at[me], tag_ref.at[me], own_sem.at[3]),
    ]
    for copy in local:
        copy.start()
    pl.semaphore_wait(barrier, devices - 1)
    peers(n_samp, samp, lambda to: note_copy(to, samp).start())
    peers(n_samp, samp, lambda to: bin_copy(to, samp).start())
    order = sorted(range(1, n_cent), key=lambda b: (b < n_cent // 2, b)) + [0]
    for b in order:
        to_plane = flip(cent, b, n_cent)
        loop(
            1 if b == 0 else 0, n_samp,
            lambda k: direct_copy(((samp + k) % n_samp) * n_cent + to_plane, me).start(),
        )
    peers(devices, me, lambda to: tag_copy(to, me).start())
    for copy in local:
        copy.wait()

    peers(n_samp, samp, lambda j: note_copy(j, j).wait_recv())
    peers(n_samp, samp, lambda j: bin_copy(j, j).wait_recv())
    code = jnp.concatenate(
        [note_ref[j] + note_ref[j + 1] for j in range(0, n_samp, 2)], axis=1
    ).astype(I32)
    tag = code % LANES
    to_cent = code // LANES
    lane_hot = ((iota((n_cent, held), 0) == to_cent) & (tag > 0)).astype(F32)
    place = column_sum(lane_hot * dot(lane_hot.astype(BF), upper_ref[0:held, 0:held])).astype(I32)
    fits = place < jnp.where(to_cent == cent, HALF, lane_rows)
    crowded = jnp.maximum(
        crowded, jnp.max(jnp.where((tag > 0) & jnp.logical_not(fits), 1.0, 0.0), axis=1, keepdims=True)
    )
    fits = fits & (tag > 0)
    hot = (iota((late_slots, held), 0) == jnp.where(fits, to_cent * HALF + place, -1)).astype(BF)
    lane_out_ref[...] = (
        dot(hot, bin_ref[...].reshape(held, width)).astype(BF).reshape(n_cent, HALF, width)
    )
    which = iota((16, held), 0)
    at = iota((16, held), 1)
    pieces = jnp.where(
        which == 0, tag, jnp.where(which == 1, at % HALF, jnp.where(which == 2, at // HALF, 0))
    ).astype(F32).astype(BF)
    for c in range(n_cent):
        seat = jnp.where(fits & (to_cent == c), (cent % 2) * HALF + place, -1)
        marks = row_dot(pieces, (iota((LANES, held), 0) == seat).astype(BF))
        mark_out_ref[c] = marks[0:1, :] + LANES * (marks[1:2, :] + HALF * marks[2:3, :])
    local = [
        pltpu.make_async_copy(lane_out_ref.at[cent], lane_ref.at[cent], own_sem.at[0]),
        pltpu.make_async_copy(mark_out_ref.at[cent], mark_ref.at[cent], own_sem.at[1]),
    ]
    for copy in local:
        copy.start()
    for b in order[:-1]:
        lane_copy(flip(cent, b, n_cent), cent).start()
    for b in order[:-1]:
        mark_copy(flip(cent, b, n_cent), cent).start()
    for copy in local:
        copy.wait()

    def columns(tags, at):
        for start in range(0, tags.shape[1], LANES):
            chunk = jnp.broadcast_to(tags[:, start:start + LANES], (LANES, LANES))
            col_ref[at + start:at + start + LANES, :] = jnp.transpose(chunk)

    def score(lines, at, fresh, tags):
        gram = row_dot(lines, fresh)
        left = col_ref[at:at + lines.shape[0], :]
        same = jnp.concatenate([left] * (tags.shape[1] // LANES), axis=1) == tags
        near_by = jnp.where(same, jnp.exp(SHARPNESS * (gram - 1.0)), 0.0)
        return column_sum(jnp.where(same, gram, 0.0)), column_sum(near_by)

    peers(devices, me, lambda j: tag_copy(j, j).wait_recv())
    tags = []
    for start in range(0, devices, pack):
        total = tag_ref[start]
        for j in range(start + 1, start + pack):
            total = total + tag_ref[j]
        tags.append(total)
    tags = jnp.concatenate(tags, axis=1)
    columns(tags, 0)
    hits = (iota((per_owner, slots), 0) + 1).astype(F32) == tags
    member_hot = hits.astype(BF)
    peers(devices, me, lambda j: direct_copy(j, j).wait_recv())
    block = 2 * LANES
    step = block // quota
    similar = jnp.zeros((1, slots), F32)
    density = jnp.zeros((1, slots), F32)
    x = x_ref[...].reshape(slots, width)
    for start in range(0, slots, block):
        lines = x_ref[start // quota:start // quota + step].reshape(block, width)
        more = score(lines, start, x, tags)
        similar = similar + more[0]
        density = density + more[1]
    sums = dot(member_hot, x)

    loop(1, n_cent, lambda k: mark_copy((cent + k) % n_cent, (cent + k) % n_cent).wait_recv())
    code = jnp.concatenate(
        [mark_ref[j] + mark_ref[j + 1] for j in range(0, n_cent, 2)], axis=1
    ).astype(I32)
    late_tags = (code % LANES).astype(F32)
    late_at = (code // LANES) % HALF
    late_from = (code // (LANES * HALF)) * n_cent + iota((1, late_slots), 1) // HALF
    columns(late_tags, slots)
    late_hits = (iota((per_owner, late_slots), 0) + 1).astype(F32) == late_tags
    loop(1, n_cent, lambda k: lane_copy((cent + k) % n_cent, (cent + k) % n_cent).wait_recv())
    late = lane_ref[...].reshape(late_slots, width)
    sums = sums + dot(late_hits.astype(BF), late)
    inverse = lax.rsqrt(jnp.sum(sums * sums, axis=1, keepdims=True) + EPSILON)

    def fold_out(value, target):
        for i in range(width // LANES):
            turn_ref[pl.ds(i, per_owner, stride=width // LANES), :] = value[:, i * LANES:(i + 1) * LANES]
        target[...] = turn_ref[...].astype(BF).reshape(span, wide, LANES)

    fold_out(sums * inverse, cent_out_ref)
    peers(span, mine, lambda to: cent_copy(to, mine).start())
    more = score(late, slots, x, tags)
    similar = similar + more[0]
    density = density + more[1]
    late_similar, late_density = score(late, slots, late, late_tags)
    for start in range(0, slots, block):
        lines = x_ref[start // quota:start // quota + step].reshape(block, width)
        more = score(lines, start, late, late_tags)
        late_similar = late_similar + more[0]
        late_density = late_density + more[1]

    def weigh(valid, hit, alike, close):
        scale = column_sum(jnp.where(hit, inverse, 0.0))
        return jnp.where(
            valid, jnp.exp(1.0 - alike * scale) / jnp.where(valid, close, 1.0), 0.0
        )

    weight = weigh(tags > 0.0, hits, similar, density)
    late_weight = weigh(late_tags > 0.0, late_hits, late_similar, late_density)
    mixed = dot(jnp.where(hits, weight, 0.0).astype(BF), x) + dot(
        jnp.where(late_hits, late_weight, 0.0).astype(BF), late
    )
    fold_out(
        mixed * lax.rsqrt(jnp.sum(mixed * mixed, axis=1, keepdims=True) + EPSILON), rep_out_ref
    )
    peers(span, mine, lambda to: rep_copy(to, mine).start())

    def halves(value):
        high = value.astype(BF)
        return jnp.concatenate([high, (value - high.astype(F32)).astype(BF)], axis=0)

    first = jnp.where(iota((devices, slots), 1) // quota == iota((devices, slots), 0), weight, 0.0)
    second = jnp.where(late_from == iota((devices, late_slots), 0), late_weight, 0.0)
    spread = row_dot(
        halves(first), (iota((LANES, slots), 1) % quota == iota((LANES, slots), 0)).astype(BF)
    ) + row_dot(halves(second), (HALF + late_at == iota((LANES, late_slots), 0)).astype(BF))
    flag = jnp.where((iota((1, LANES), 1) == LANES - 1) & (crowded > 0.0), SPILL, 0.0)
    weight_ref[:, 0, :] = spread[0:devices, :] + spread[devices:, :] + flag
    peers(devices, me, lambda to: weight_copy(to, me).start())
    local = [
        pltpu.make_async_copy(cent_out_ref.at[mine], cent_ref.at[mine], own_sem.at[0]),
        pltpu.make_async_copy(rep_out_ref.at[mine], rep_ref.at[mine], own_sem.at[1]),
        pltpu.make_async_copy(weight_ref.at[me], back_ref.at[me], own_sem.at[2]),
    ]
    for copy in local:
        copy.start()

    peers(n_samp, samp, lambda to: note_copy(to, samp).wait_send())
    peers(n_samp, samp, lambda to: bin_copy(to, samp).wait_send())
    peers(devices, me, lambda to: direct_copy(to, me).wait_send())
    peers(devices, me, lambda to: tag_copy(to, me).wait_send())
    peers(n_cent, cent, lambda to: lane_copy(to, cent).wait_send())
    peers(n_cent, cent, lambda to: mark_copy(to, cent).wait_send())
    peers(span, mine, lambda to: cent_copy(to, mine).wait_send())
    peers(span, mine, lambda to: rep_copy(to, mine).wait_send())
    peers(devices, me, lambda to: weight_copy(to, me).wait_send())
    for copy in local:
        copy.wait()
    peers(span, mine, lambda j: cent_copy(j, j).wait_recv())
    peers(span, mine, lambda j: rep_copy(j, j).wait_recv())
    peers(devices, me, lambda j: weight_copy(j, j).wait_recv())


def finish_kernel(
    per_owner, cent_ref, rep_ref, back_ref, meta_ref, centroid_ref, representative_ref, keep_ref, top_ref, turn_ref
):
    span, wide, _ = cent_ref.shape
    each = per_owner // span
    chunks = wide // each
    devices = back_ref.shape[0]
    rows = meta_ref.shape[1]
    back = back_ref[:, 0, :]
    top_ref[0, 0] = jnp.max(back)
    rank = iota((per_owner, per_owner), 0)
    is_high = rank >= per_owner // 2
    fold = jnp.where(is_high, per_owner - 1 - rank, rank)
    source = (fold % span) * each + fold // span + jnp.where(is_high, each // 2, 0)
    order = (iota((per_owner, per_owner), 1) == source).astype(BF)
    for got, out in ((cent_ref, centroid_ref), (rep_ref, representative_ref)):
        turn_ref[...] = got[...].reshape(span * wide, LANES).astype(F32)
        flat = jnp.concatenate(
            [turn_ref[pl.ds(i, per_owner, stride=chunks), :] for i in range(chunks)], axis=1
        )
        out[...] = dot(order, flat.astype(BF))
    meta = meta_ref[...]
    dest_hot = (iota((devices, rows), 0) == meta[0:1, :]).astype(F32)
    spread = lax.dot_general(
        back, dest_hot, (((0,), (0,)), ((), ())),
        preferred_element_type=F32, precision=lax.Precision.HIGHEST,
    )
    hit = iota((LANES, rows), 0) == meta[1:2, :]
    keep_ref[...] = column_sum(jnp.where(hit, spread, 0.0))


def all_pairs(arrived, arrived_tags, validity, block_size):
    slot_count, feature_width = arrived.shape
    block_count = slot_count // block_size

    def score_block(pieces):
        block_rows, block_tags = pieces
        gram = jnp.einsum("rd,qd->rq", block_rows, arrived, preferred_element_type=jnp.float32)
        same_cluster = (block_tags[:, None] == arrived_tags[None, :]) & validity[None, :]
        similar = jnp.sum(jnp.where(same_cluster, gram, 0.0), axis=1)
        density = jnp.sum(jnp.where(same_cluster, jnp.exp(SHARPNESS * (gram - 1.0)), 0.0), axis=1)
        return (similar, density)

    similar, density = lax.map(
        score_block,
        (
            arrived.reshape(block_count, block_size, feature_width),
            arrived_tags.reshape(block_count, block_size),
        ),
    )
    return (similar.reshape(slot_count), density.reshape(slot_count))


def full_capacity(embeddings, assignment, owner_map):
    row_count, feature_width = embeddings.shape
    devices = lax.axis_size("samp") * lax.axis_size("cent")
    clusters = owner_map.shape[0]
    per_owner = clusters // devices
    capacity = 4 * row_count // devices
    slot_count = devices * capacity
    unit_rows = (
        embeddings * lax.rsqrt(jnp.sum(embeddings * embeddings, axis=1, keepdims=True) + EPSILON)
    ).astype(jnp.bfloat16)
    destination = owner_map[assignment]
    cluster_order = jnp.argsort(owner_map, stable=True)
    position = (
        jnp.zeros((clusters,), jnp.int32)
        .at[cluster_order]
        .set(jnp.arange(clusters, dtype=jnp.int32))
    )
    local_rank = position[assignment] - destination * per_owner
    dest_onehot = (destination[:, None] == jnp.arange(devices, dtype=jnp.int32)[None, :]).astype(
        jnp.int32
    )
    within_rank = jnp.sum(jnp.cumsum(dest_onehot, axis=0) * dest_onehot, axis=1) - 1
    slot_index = destination * capacity + within_rank
    outgoing = jnp.zeros((slot_count, feature_width), jnp.bfloat16).at[slot_index].set(unit_rows)
    labels = (
        jnp.zeros((slot_count,), jnp.bfloat16)
        .at[slot_index]
        .set((local_rank + 1).astype(jnp.bfloat16))
    )
    arrived, arrived_labels = (
        lax.all_to_all(outgoing, ("samp", "cent"), split_axis=0, concat_axis=0, tiled=True),
        lax.all_to_all(labels, ("samp", "cent"), split_axis=0, concat_axis=0, tiled=True),
    )
    arrived_tags = arrived_labels.astype(jnp.int32) - 1
    validity = arrived_tags >= 0
    block_size = min(512, slot_count)
    similar, density = all_pairs(arrived, arrived_tags, validity, block_size)
    member = arrived_tags[None, :] == jnp.arange(per_owner, dtype=jnp.int32)[:, None]
    member_bf = member.astype(jnp.bfloat16)
    cluster_sums = jnp.dot(member_bf, arrived, preferred_element_type=jnp.float32)
    inverse_norm = lax.rsqrt(jnp.sum(cluster_sums * cluster_sums, axis=1) + EPSILON)
    row_scale = jnp.sum(member.astype(jnp.float32) * inverse_norm[:, None], axis=0)
    spread = 1.0 - similar * row_scale
    weight = jnp.where(validity, jnp.exp(spread) / jnp.where(validity, density, 1.0), 0.0)
    weighted = jnp.dot(
        member_bf * weight.astype(jnp.bfloat16)[None, :],
        arrived,
        preferred_element_type=jnp.float32,
    )
    centroid = cluster_sums * inverse_norm[:, None]
    representative = weighted * lax.rsqrt(
        jnp.sum(weighted * weighted, axis=1, keepdims=True) + EPSILON
    )
    returned = lax.all_to_all(weight, ("samp", "cent"), split_axis=0, concat_axis=0, tiled=True)
    keep_weight = returned[slot_index]
    return (centroid, representative, keep_weight)


def on_device(embeddings, assignment, owner_map):
    rows, width = embeddings.shape
    n_samp = lax.axis_size("samp")
    n_cent = lax.axis_size("cent")
    devices = n_samp * n_cent
    clusters = owner_map.shape[0]
    per_owner = clusters // devices
    groups = max(1, 2 * devices // per_owner)
    quota = -(-rows // devices // 16) * 16
    bin_rows = 48
    lane_rows = 56
    span = devices // groups
    wide = per_owner // span * (width // LANES)
    slots = devices * quota
    late_slots = n_cent * HALF
    depth = max(rows, n_samp * HALF)
    vmem = pl.BlockSpec(memory_space=pltpu.VMEM)
    anywhere = pl.BlockSpec(memory_space=pl.ANY)
    shape = jax.ShapeDtypeStruct
    dma = pltpu.SemaphoreType.DMA
    centroid, representative, back, meta = pl.pallas_call(
        functools.partial(
            dedup_kernel, n_samp, n_cent, groups, per_owner, quota, bin_rows, lane_rows
        ),
        out_shape=(
            shape((span, wide, LANES), BF),
            shape((span, wide, LANES), BF),
            shape((devices, 1, LANES), F32),
            shape((8, rows), I32),
        ),
        in_specs=[anywhere, vmem, vmem],
        out_specs=(vmem,) * 4,
        scratch_shapes=[
            pltpu.VMEM((rows, width), F32),
            pltpu.VMEM((depth, depth), BF),
            pltpu.VMEM((devices, quota, width), BF),
            pltpu.VMEM((devices, quota, width), BF),
            pltpu.VMEM((devices, 1, LANES), F32),
            pltpu.VMEM((devices, 1, LANES), F32),
            pltpu.VMEM((n_samp, bin_rows, width), BF),
            pltpu.VMEM((n_samp, HALF, width), BF),
            pltpu.VMEM((n_samp, 1, LANES), F32),
            pltpu.VMEM((n_samp, 1, LANES), F32),
            pltpu.VMEM((n_cent, HALF, width), BF),
            pltpu.VMEM((n_cent, HALF, width), BF),
            pltpu.VMEM((n_cent, 1, LANES), F32),
            pltpu.VMEM((n_cent, 1, LANES), F32),
            pltpu.VMEM((slots + late_slots, LANES), F32),
            pltpu.VMEM((span * wide, LANES), F32),
            pltpu.VMEM((span, wide, LANES), BF),
            pltpu.VMEM((span, wide, LANES), BF),
            pltpu.VMEM((devices, 1, LANES), F32),
            dma((4,)), dma((4,)),
            dma((devices,)), dma((devices,)), dma((devices,)), dma((devices,)),
            dma((n_samp,)), dma((n_samp,)), dma((n_samp,)), dma((n_samp,)),
            dma((n_cent,)), dma((n_cent,)), dma((n_cent,)), dma((n_cent,)),
            dma((span,)), dma((span,)), dma((span,)), dma((span,)),
            dma((devices,)), dma((devices,)),
        ],
        compiler_params=pltpu.CompilerParams(collective_id=0, has_side_effects=True),
        name="dedup",
    )(embeddings, assignment.reshape(1, rows), owner_map.reshape(clusters // LANES, LANES))
    centroid, representative, keep, top = pl.pallas_call(
        functools.partial(finish_kernel, per_owner),
        out_shape=(
            shape((per_owner, width), F32),
            shape((per_owner, width), F32),
            shape((1, rows), F32),
            shape((1, 1), F32),
        ),
        in_specs=[vmem] * 4,
        out_specs=(vmem, vmem, vmem, pl.BlockSpec(memory_space=pltpu.SMEM)),
        scratch_shapes=[pltpu.VMEM((span * wide, LANES), F32)],
        name="finish",
    )(centroid, representative, back, meta)
    keep = keep.reshape(rows)

    def fast(embeddings, assignment, owner_map, centroid, representative, keep):
        return centroid, representative, keep

    def slow(embeddings, assignment, owner_map, centroid, representative, keep):
        return full_capacity(embeddings, assignment, owner_map)

    spilled = top[0, 0] >= SPILL
    return lax.cond(
        spilled, slow, fast, embeddings, assignment, owner_map, centroid, representative, keep
    )


def solution(mesh):
    in_specs = (P(("samp", "cent"), None), P(("samp", "cent")), P())
    out_specs = (P(("samp", "cent"), None), P(("samp", "cent"), None), P(("samp", "cent")))
    return jax.shard_map(
        on_device, mesh=mesh, in_specs=in_specs, out_specs=out_specs, check_vma=False
    )
```

time: 87.8 us -> 59.1 us (0.67)
  Pallas kernels: 84.6 us -> 57.2 us
  local copies, waits for them, and re-layouts: 1.41 us -> 0 us
    pallas_call x3 -> x2, Pallas kernels: 84.6 us -> 57.2 us  [the longest x1 55.2 us: on_device(): pl.pallas_call(functools.partial(dedup_kernel, n_samp, n_cent, groups, pe...]
    unnamed x4 -> x0, local copies, waits for them, and re-layouts: 1.41 us -> none
where the time goes in v1:
time: 59.1 us; the launch traced here: 58.8 us
  Pallas kernels  57.2 us (97%)
  between operations  1.37 us (2%)
    pallas_call x1, Pallas kernels, on_device(): pl.pallas_call(functools.partial(dedup_kernel, n_samp, n_cent, groups, pe...  55.2 us
    pallas_call x1, Pallas kernels, on_device(): pl.pallas_call(functools.partial(finish_kernel, per_owner), out_shape=(sh...  2.06 us

profile of v1, /device:TPU:0, one launch (start us, length us, event | category | flops | bytes accessed | tf_op | source)
XLA Modules:
  0.0 58.8 jit_solution(15865208185380062719)
XLA Ops:
  0.6 55.2 %dedup.1 = (bf16[32,16,128]{2,1,0:T(8,128)(2,1)}, bf16[32,16,128]{2,1,0:T(8,128)(2,1)}, f32[32,1,128]{2,1,0:T(1,128)}, s32[8,512]{1,0:T(8,128)}) custom-call(f32[512,1024]{1,0:T(8,128)} %emb_hbm.1, s32[1,512]{1,0:T(1,128)} %bitcast.63, s32[16,128]{1,0:T(8,128)} %bitcast.52), custom_call_target="tpu_custom_call" | custom-call | tf_op jit(solution)/shard_map/dedup/pallas_call | solution.py:523
  55.8 2.1 %finish.1 = (f32[64,1024]{1,0:T(8,128)}, f32[64,1024]{1,0:T(8,128)}, f32[1,512]{1,0:T(1,128)}, f32[1,1]{1,0:T(1,128)}) custom-call(bf16[32,16,128]{2,1,0:T(8,128)(2,1)} %get-tuple-element.136.cent_ref, bf16[32,16,128]{2,1,0:T(8,128)(2,1)} %get-tuple-element.137.rep_ref, f32[32,1,128]{2,1,0:T(1,128)} %get-tuple-element.138.back_ref, ...), custom_call_target="tpu_custom_call" | custom-call | tf_op jit(solution)/shard_map/finish/pallas_call | solution.py:565
  58.4 0.2 conditional.1

commit v2 on v1

v2 whole, which is shorter than its diff:
```python
import functools

import jax
import jax.numpy as jnp
from jax import lax
from jax.experimental import pallas as pl
from jax.experimental.pallas import tpu as pltpu
from jax.sharding import PartitionSpec as P

EPSILON = 1e-06
SHARPNESS = 8.0
LANES = 128
HALF = LANES // 2
SPILL = 65536.0
BF = jnp.bfloat16
F32 = jnp.float32
I32 = jnp.int32
MESH = pl.DeviceIdType.MESH


def iota(shape, axis):
    return lax.broadcasted_iota(jnp.int32, shape, axis)


def row_dot(a, b):
    return lax.dot_general(a, b, (((1,), (1,)), ((), ())), preferred_element_type=F32)


def dot(a, b):
    return jnp.dot(a, b, preferred_element_type=F32)


def column_sum(a):
    return jnp.sum(a, axis=0, keepdims=True)


def flip(index, bits):
    step = 1
    while step <= bits:
        if bits & step:
            index = index + step * (1 - 2 * ((index // step) % 2))
        step *= 2
    return index


def plane_order(n_cent):
    return sorted(range(1, n_cent), key=lambda b: (b < n_cent // 2, b)) + [0]


def dedup_kernel(
    n_samp, n_cent, groups, per_owner, quota, bin_rows, lane_rows,
    emb_hbm, assign_ref, owner_ref, cent_ref, rep_ref, back_ref, meta_ref,
    emb_ref, upper_ref, direct_ref, x_ref, tag_out_ref, tag_ref, bin_out_ref, bin_ref, note_out_ref, note_ref,
    lane_out_ref, mark_out_ref, mark_ref, col_ref, turn_ref, cent_out_ref, rep_out_ref, weight_ref,
    load_sem, own_sem, direct_out, direct_in, tag_out, tag_in, bin_out, bin_in, note_out, note_in,
    lane_out, lane_in, mark_out, mark_in, cent_send, cent_recv, rep_send, rep_recv, weight_out, weight_in,
):
    samp = lax.axis_index("samp")
    cent = lax.axis_index("cent")
    devices = n_samp * n_cent
    rows, width = emb_ref.shape
    table_rows = owner_ref.shape[0]
    span = devices // groups
    near = n_cent // groups
    each = per_owner // span
    wide = each * (width // LANES)
    slots = devices * quota
    late_slots = n_cent * HALF
    held = n_samp * HALF
    order = plane_order(n_cent)
    samps = [flip(samp, a) for a in range(n_samp)]
    cents = [flip(cent, b) for b in range(n_cent)]
    peers = [
        (i * n_samp + a, (samps[a], cents[b]))
        for i, b in enumerate(order)
        for a in range(n_samp)
        if a or b
    ]
    own = order.index(0) * n_samp

    def remote(source, target, sent, received, device):
        return pltpu.make_async_remote_copy(
            source, target, sent, received, device_id=device, device_id_type=MESH
        )

    part = rows // load_sem.shape[0]
    loads = [
        pltpu.make_async_copy(
            emb_hbm.at[pl.ds(i * part, part)], emb_ref.at[pl.ds(i * part, part)], load_sem.at[i]
        )
        for i in range(load_sem.shape[0])
    ]
    for copy in loads:
        copy.start()
    barrier = pltpu.get_barrier_semaphore()
    for _, device in peers:
        pl.semaphore_signal(barrier, inc=1, device_id=device, device_id_type=MESH)

    bin_ref[:, bin_rows:, :] = jnp.zeros((n_samp, HALF - bin_rows, width), BF)
    for b in range(1, n_cent):
        x_ref[slots + b * HALF + lane_rows:slots + (b + 1) * HALF, :] = jnp.zeros(
            (HALF - lane_rows, width), BF
        )
    upper_ref[...] = (iota(upper_ref.shape, 0) < iota(upper_ref.shape, 1)).astype(BF)

    owner = owner_ref[...]
    owner_hot = (iota((table_rows, devices, LANES), 1) == owner[:, None, :]).astype(F32)
    before = dot(
        owner_hot.reshape(table_rows * devices, LANES).astype(BF), upper_ref[0:LANES, 0:LANES]
    ).reshape(table_rows, devices, LANES)
    base = jnp.zeros((devices, 1), F32)
    ranks = []
    for i in range(table_rows):
        ranks.append(column_sum(owner_hot[i] * (before[i] + base)))
        base = base + jnp.sum(owner_hot[i], axis=1, keepdims=True)
    table = jnp.concatenate([owner.astype(F32)] + ranks, axis=0).astype(BF)
    assign = assign_ref[...]
    found = dot(table, (iota((LANES, rows), 0) == assign % LANES).astype(BF))
    line = iota((table_rows, rows), 0) == assign // LANES
    owned = column_sum(jnp.where(line, found[0:table_rows, :], 0.0)).astype(I32)
    rank = column_sum(jnp.where(line, found[table_rows:, :], 0.0)).astype(I32)
    is_high = rank >= per_owner // 2
    fold = jnp.where(is_high, per_owner - 1 - rank, rank)
    place = fold % span
    own_cent = owned % n_cent
    to_samp = place // near
    to_cent = (own_cent // near) * near + place % near
    chosen = fold // span + jnp.where(is_high, each // 2, 0)
    apart = ((owned // n_cent) ^ to_samp) * near + (own_cent ^ to_cent)
    tag = (apart * each + chosen + 1).astype(F32)
    to_samp = to_samp ^ samp
    to_cent = to_cent ^ cent
    dest = to_samp
    for i, b in enumerate(order):
        dest = dest + jnp.where(to_cent == b, i * n_samp, 0)

    upper = upper_ref[0:rows, 0:rows]
    dest_hot = (iota((devices, rows), 0) == dest).astype(F32)
    within = column_sum(dest_hot * dot(dest_hot.astype(BF), upper)).astype(I32)
    is_late = within >= quota
    late_hot = ((iota((n_samp, rows), 0) == to_samp) & is_late).astype(F32)
    place = column_sum(late_hot * dot(late_hot.astype(BF), upper)).astype(I32)
    crowded = jnp.max(jnp.where(is_late & (place >= bin_rows), 1.0, 0.0), axis=1, keepdims=True)
    meta_ref[...] = jnp.where(
        iota((8, rows), 0) == 0, dest, jnp.where(is_late, HALF + place, within)
    )

    for copy in loads:
        copy.wait()
    emb = emb_ref[...]
    unit = (emb * lax.rsqrt(jnp.sum(emb * emb, axis=1, keepdims=True) + EPSILON)).astype(BF)
    direct_seat = jnp.where(is_late, -1, dest * quota + within)
    block = 2 * LANES

    def pack_direct(start):
        hot = (iota((block, rows), 0) + start == direct_seat).astype(BF)
        direct_ref[start:start + block, :] = dot(hot, unit).astype(BF)

    def direct_copy(slot, device):
        at = pl.ds(slot * quota, quota)
        return remote(direct_ref.at[at], x_ref.at[at], direct_out.at[slot], direct_in.at[slot], device)

    def tag_copy(slot, device):
        return remote(tag_out_ref.at[slot], tag_ref.at[slot], tag_out.at[slot], tag_in.at[slot], device)

    def bin_copy(a):
        return remote(
            bin_out_ref.at[a], bin_ref.at[a, pl.ds(0, bin_rows)], bin_out.at[a], bin_in.at[a], (samps[a], cent)
        )

    def note_copy(a):
        return remote(note_out_ref.at[a], note_ref.at[a], note_out.at[a], note_in.at[a], (samps[a], cent))

    def lane_copy(b):
        return remote(
            lane_out_ref.at[b, pl.ds(0, lane_rows)], x_ref.at[pl.ds(slots + b * HALF, lane_rows)],
            lane_out.at[b], lane_in.at[b], (samp, cents[b]),
        )

    def mark_copy(b):
        return remote(mark_out_ref.at[b], mark_ref.at[b], mark_out.at[b], mark_in.at[b], (samp, cents[b]))

    def cent_copy(slot, device):
        return remote(cent_out_ref.at[slot], cent_ref.at[slot], cent_send.at[slot], cent_recv.at[slot], device)

    def rep_copy(slot, device):
        return remote(rep_out_ref.at[slot], rep_ref.at[slot], rep_send.at[slot], rep_recv.at[slot], device)

    def weight_copy(slot, device):
        return remote(weight_ref.at[slot], back_ref.at[slot], weight_out.at[slot], weight_in.at[slot], device)

    owners = [
        (a * near + b, (samps[a], cents[b]))
        for b in sorted(range(near), key=lambda b: (b < near // 2, b))
        for a in range(n_samp)
        if a or b
    ]

    def send_direct(start):
        for slot, device in peers:
            if start <= slot * quota < start + block:
                direct_copy(slot, device).start()

    pack_direct(0)
    pl.semaphore_wait(barrier, devices - 1)
    send_direct(0)

    seat = jnp.where(is_late & (place < bin_rows), (to_samp % 2) * HALF + place, -1)
    notes = row_dot(
        jnp.concatenate([late_hot * tag, late_hot * to_cent.astype(F32)], axis=0).astype(BF),
        (iota((LANES, rows), 0) == seat).astype(BF),
    )
    note_out_ref[:, 0, :] = notes[0:n_samp, :] + LANES * notes[n_samp:, :]
    seat = jnp.where(is_late & (place < bin_rows), to_samp * bin_rows + place, -1)
    hot = (iota((n_samp * bin_rows, rows), 0) == seat).astype(BF)
    bin_out_ref[...] = dot(hot, unit).astype(BF).reshape(n_samp, bin_rows, width)
    for a in range(1, n_samp):
        note_copy(a).start()
    for a in range(1, n_samp):
        bin_copy(a).start()
    for start in range(block, slots, block):
        pack_direct(start)
        send_direct(start)
    pack = LANES // quota
    seat = jnp.where(is_late, -1, (dest % pack) * quota + within)
    tag_out_ref[:, 0, :] = row_dot(
        (dest_hot * tag).astype(BF), (iota((LANES, rows), 0) == seat).astype(BF)
    )
    for slot, device in peers:
        tag_copy(slot, device).start()
    mine = pl.ds(own * quota, quota)
    local = [
        pltpu.make_async_copy(bin_out_ref.at[0], bin_ref.at[0, pl.ds(0, bin_rows)], own_sem.at[0]),
        pltpu.make_async_copy(note_out_ref.at[0], note_ref.at[0], own_sem.at[1]),
        pltpu.make_async_copy(direct_ref.at[mine], x_ref.at[mine], own_sem.at[2]),
        pltpu.make_async_copy(tag_out_ref.at[own], tag_ref.at[own], own_sem.at[3]),
    ]
    for copy in local:
        copy.start()
    for copy in local:
        copy.wait()

    for a in range(1, n_samp):
        note_copy(a).wait_recv()
    code = jnp.concatenate(
        [note_ref[j] + note_ref[j + 1] for j in range(0, n_samp, 2)], axis=1
    ).astype(I32)
    tag = code % LANES
    to_cent = code // LANES
    lane_hot = ((iota((n_cent, held), 0) == to_cent) & (tag > 0)).astype(F32)
    place = column_sum(lane_hot * dot(lane_hot.astype(BF), upper_ref[0:held, 0:held])).astype(I32)
    fits = place < jnp.where(to_cent == 0, HALF, lane_rows)
    crowded = jnp.maximum(
        crowded, jnp.max(jnp.where((tag > 0) & jnp.logical_not(fits), 1.0, 0.0), axis=1, keepdims=True)
    )
    fits = fits & (tag > 0)
    which = iota((16, held), 0)
    at = iota((16, held), 1)
    pieces = jnp.where(
        which == 0, tag, jnp.where(which == 1, at % HALF, jnp.where(which == 2, at // HALF, 0))
    ).astype(F32).astype(BF)
    for b in range(n_cent):
        seat = jnp.where(fits & (to_cent == b), (b % 2) * HALF + place, -1)
        marks = row_dot(pieces, (iota((LANES, held), 0) == seat).astype(BF))
        mark_out_ref[b] = marks[0:1, :] + LANES * (marks[1:2, :] + HALF * marks[2:3, :])
    hot = (iota((late_slots, held), 0) == jnp.where(fits, to_cent * HALF + place, -1)).astype(BF)
    for a in range(1, n_samp):
        bin_copy(a).wait_recv()
    lane_out_ref[...] = (
        dot(hot, bin_ref[...].reshape(held, width)).astype(BF).reshape(n_cent, HALF, width)
    )
    for b in order[:-1]:
        mark_copy(b).start()
    for b in order[:-1]:
        lane_copy(b).start()
    local = [
        pltpu.make_async_copy(lane_out_ref.at[0], x_ref.at[pl.ds(slots, HALF)], own_sem.at[0]),
        pltpu.make_async_copy(mark_out_ref.at[0], mark_ref.at[0], own_sem.at[1]),
    ]
    for copy in local:
        copy.start()
    for copy in local:
        copy.wait()

    def columns(tags, at):
        for start in range(0, tags.shape[1], LANES):
            chunk = jnp.broadcast_to(tags[:, start:start + LANES], (LANES, LANES))
            col_ref[at + start:at + start + LANES, :] = jnp.transpose(chunk)

    def score(low, high, fresh, tags):
        alike = jnp.zeros(tags.shape, F32)
        close = jnp.zeros(tags.shape, F32)
        for start in range(low, high, block):
            end = min(start + block, high)
            gram = row_dot(x_ref[start:end, :], fresh)
            left = col_ref[start:end, :]
            same = jnp.concatenate([left] * (tags.shape[1] // LANES), axis=1) == tags
            alike = alike + column_sum(jnp.where(same, gram, 0.0))
            close = close + column_sum(jnp.where(same, jnp.exp(SHARPNESS * (gram - 1.0)), 0.0))
        return alike, close

    def hit(tags):
        return (iota((per_owner, tags.shape[1]), 0) + 1).astype(F32) == tags

    for slot, device in peers:
        tag_copy(slot, device).wait_recv()
    tags = []
    for start in range(0, devices, pack):
        total = tag_ref[start]
        for j in range(start + 1, start + pack):
            total = total + tag_ref[j]
        tags.append(total)
    tags = jnp.concatenate(tags, axis=1)
    columns(tags, 0)
    for slot, device in peers:
        direct_copy(slot, device).wait_recv()
    x = x_ref[0:slots, :]
    similar, density = score(0, slots, x, tags)
    sums = dot(hit(tags).astype(BF), x)

    for b in range(1, n_cent):
        mark_copy(b).wait_recv()
    sources = []
    columns_of = []
    for b in range(0, n_cent, 2):
        code = (mark_ref[b] + mark_ref[b + 1]).astype(I32)
        fresh_tags = (code % LANES).astype(F32)
        columns_of.append(HALF + (code // LANES) % HALF)
        lane = iota((1, LANES), 1)
        sources.append(
            code // (LANES * HALF)
            + n_samp * jnp.where(lane < HALF, order.index(b), order.index(b + 1))
        )
        at = slots + b * HALF
        columns(fresh_tags, at)
        for c in (b, b + 1):
            if c:
                lane_copy(c).wait_recv()
        fresh = x_ref[at:at + LANES, :]
        sums = sums + dot(hit(fresh_tags).astype(BF), fresh)
        if b == n_cent - 2:
            inverse = lax.rsqrt(jnp.sum(sums * sums, axis=1, keepdims=True) + EPSILON)
        alike, close = score(0, at + LANES, fresh, fresh_tags)
        more_alike, more_close = score(at, at + LANES, x_ref[0:at, :], tags)
        similar = jnp.concatenate([similar + more_alike, alike], axis=1)
        density = jnp.concatenate([density + more_close, close], axis=1)
        tags = jnp.concatenate([tags, fresh_tags], axis=1)

    def fold_out(value, target):
        for i in range(width // LANES):
            turn_ref[pl.ds(i, per_owner, stride=width // LANES), :] = value[:, i * LANES:(i + 1) * LANES]
        target[...] = turn_ref[...].astype(BF).reshape(span, wide, LANES)

    fold_out(sums * inverse, cent_out_ref)
    for slot, device in owners:
        cent_copy(slot, device).start()
    hits = hit(tags)
    valid = tags > 0.0
    scale = column_sum(jnp.where(hits, inverse, 0.0))
    weight = jnp.where(
        valid, jnp.exp(1.0 - similar * scale) / jnp.where(valid, density, 1.0), 0.0
    )
    mixed = dot(jnp.where(hits, weight, 0.0).astype(BF), x_ref[...])
    fold_out(
        mixed * lax.rsqrt(jnp.sum(mixed * mixed, axis=1, keepdims=True) + EPSILON), rep_out_ref
    )
    for slot, device in owners:
        rep_copy(slot, device).start()

    lane = iota((1, slots), 1)
    sources = jnp.concatenate([lane // quota] + sources, axis=1)
    columns_of = jnp.concatenate([lane % quota] + columns_of, axis=1)
    spread = jnp.where(iota((devices, slots + late_slots), 0) == sources, weight, 0.0)
    high = spread.astype(BF)
    spread = row_dot(
        jnp.concatenate([high, (spread - high.astype(F32)).astype(BF)], axis=0),
        (iota((LANES, slots + late_slots), 0) == columns_of).astype(BF),
    )
    flag = jnp.where((iota((1, LANES), 1) == LANES - 1) & (crowded > 0.0), SPILL, 0.0)
    weight_ref[:, 0, :] = spread[0:devices, :] + spread[devices:, :] + flag
    for slot, device in peers:
        weight_copy(slot, device).start()
    local = [
        pltpu.make_async_copy(cent_out_ref.at[0], cent_ref.at[0], own_sem.at[0]),
        pltpu.make_async_copy(rep_out_ref.at[0], rep_ref.at[0], own_sem.at[1]),
        pltpu.make_async_copy(weight_ref.at[own], back_ref.at[own], own_sem.at[2]),
    ]
    for copy in local:
        copy.start()

    for a in range(1, n_samp):
        note_copy(a).wait_send()
        bin_copy(a).wait_send()
    for b in range(1, n_cent):
        lane_copy(b).wait_send()
        mark_copy(b).wait_send()
    for slot, device in peers:
        direct_copy(slot, device).wait_send()
        tag_copy(slot, device).wait_send()
    for copy in local:
        copy.wait()
    for slot, device in owners:
        cent_copy(slot, device).wait()
        rep_copy(slot, device).wait()
    for slot, device in peers:
        weight_copy(slot, device).wait()


def finish_kernel(
    per_owner, n_cent, cent_ref, rep_ref, back_ref, meta_ref, centroid_ref, representative_ref, keep_ref, top_ref, turn_ref
):
    span, wide, _ = cent_ref.shape
    each = per_owner // span
    chunks = wide // each
    devices = back_ref.shape[0]
    rows = meta_ref.shape[1]
    near = n_cent * span // devices
    mine = lax.axis_index("samp") * near + lax.axis_index("cent") % near
    back = back_ref[:, 0, :]
    top_ref[0, 0] = jnp.max(back)
    rank = iota((per_owner, per_owner), 0)
    is_high = rank >= per_owner // 2
    fold = jnp.where(is_high, per_owner - 1 - rank, rank)
    source = ((fold % span) ^ mine) * each + fold // span + jnp.where(is_high, each // 2, 0)
    order = (iota((per_owner, per_owner), 1) == source).astype(BF)
    for got, out in ((cent_ref, centroid_ref), (rep_ref, representative_ref)):
        turn_ref[...] = got[...].reshape(span * wide, LANES).astype(F32)
        flat = jnp.concatenate(
            [turn_ref[pl.ds(i, per_owner, stride=chunks), :] for i in range(chunks)], axis=1
        )
        out[...] = dot(order, flat.astype(BF))
    meta = meta_ref[...]
    dest_hot = (iota((devices, rows), 0) == meta[0:1, :]).astype(F32)
    spread = lax.dot_general(
        back, dest_hot, (((0,), (0,)), ((), ())),
        preferred_element_type=F32, precision=lax.Precision.HIGHEST,
    )
    hit = iota((LANES, rows), 0) == meta[1:2, :]
    keep_ref[...] = column_sum(jnp.where(hit, spread, 0.0))


def all_pairs(arrived, arrived_tags, validity, block_size):
    slot_count, feature_width = arrived.shape
    block_count = slot_count // block_size

    def score_block(pieces):
        block_rows, block_tags = pieces
        gram = jnp.einsum("rd,qd->rq", block_rows, arrived, preferred_element_type=jnp.float32)
        same_cluster = (block_tags[:, None] == arrived_tags[None, :]) & validity[None, :]
        similar = jnp.sum(jnp.where(same_cluster, gram, 0.0), axis=1)
        density = jnp.sum(jnp.where(same_cluster, jnp.exp(SHARPNESS * (gram - 1.0)), 0.0), axis=1)
        return (similar, density)

    similar, density = lax.map(
        score_block,
        (
            arrived.reshape(block_count, block_size, feature_width),
            arrived_tags.reshape(block_count, block_size),
        ),
    )
    return (similar.reshape(slot_count), density.reshape(slot_count))


def full_capacity(embeddings, assignment, owner_map):
    row_count, feature_width = embeddings.shape
    devices = lax.axis_size("samp") * lax.axis_size("cent")
    clusters = owner_map.shape[0]
    per_owner = clusters // devices
    capacity = 4 * row_count // devices
    slot_count = devices * capacity
    unit_rows = (
        embeddings * lax.rsqrt(jnp.sum(embeddings * embeddings, axis=1, keepdims=True) + EPSILON)
    ).astype(jnp.bfloat16)
    destination = owner_map[assignment]
    cluster_order = jnp.argsort(owner_map, stable=True)
    position = (
        jnp.zeros((clusters,), jnp.int32)
        .at[cluster_order]
        .set(jnp.arange(clusters, dtype=jnp.int32))
    )
    local_rank = position[assignment] - destination * per_owner
    dest_onehot = (destination[:, None] == jnp.arange(devices, dtype=jnp.int32)[None, :]).astype(
        jnp.int32
    )
    within_rank = jnp.sum(jnp.cumsum(dest_onehot, axis=0) * dest_onehot, axis=1) - 1
    slot_index = destination * capacity + within_rank
    outgoing = jnp.zeros((slot_count, feature_width), jnp.bfloat16).at[slot_index].set(unit_rows)
    labels = (
        jnp.zeros((slot_count,), jnp.bfloat16)
        .at[slot_index]
        .set((local_rank + 1).astype(jnp.bfloat16))
    )
    arrived, arrived_labels = (
        lax.all_to_all(outgoing, ("samp", "cent"), split_axis=0, concat_axis=0, tiled=True),
        lax.all_to_all(labels, ("samp", "cent"), split_axis=0, concat_axis=0, tiled=True),
    )
    arrived_tags = arrived_labels.astype(jnp.int32) - 1
    validity = arrived_tags >= 0
    block_size = min(512, slot_count)
    similar, density = all_pairs(arrived, arrived_tags, validity, block_size)
    member = arrived_tags[None, :] == jnp.arange(per_owner, dtype=jnp.int32)[:, None]
    member_bf = member.astype(jnp.bfloat16)
    cluster_sums = jnp.dot(member_bf, arrived, preferred_element_type=jnp.float32)
    inverse_norm = lax.rsqrt(jnp.sum(cluster_sums * cluster_sums, axis=1) + EPSILON)
    row_scale = jnp.sum(member.astype(jnp.float32) * inverse_norm[:, None], axis=0)
    spread = 1.0 - similar * row_scale
    weight = jnp.where(validity, jnp.exp(spread) / jnp.where(validity, density, 1.0), 0.0)
    weighted = jnp.dot(
        member_bf * weight.astype(jnp.bfloat16)[None, :],
        arrived,
        preferred_element_type=jnp.float32,
    )
    centroid = cluster_sums * inverse_norm[:, None]
    representative = weighted * lax.rsqrt(
        jnp.sum(weighted * weighted, axis=1, keepdims=True) + EPSILON
    )
    returned = lax.all_to_all(weight, ("samp", "cent"), split_axis=0, concat_axis=0, tiled=True)
    keep_weight = returned[slot_index]
    return (centroid, representative, keep_weight)


def on_device(embeddings, assignment, owner_map):
    rows, width = embeddings.shape
    n_samp = lax.axis_size("samp")
    n_cent = lax.axis_size("cent")
    devices = n_samp * n_cent
    clusters = owner_map.shape[0]
    per_owner = clusters // devices
    groups = max(1, 2 * devices // per_owner)
    quota = -(-rows // devices // 16) * 16
    bin_rows = 48
    lane_rows = 56
    span = devices // groups
    wide = per_owner // span * (width // LANES)
    slots = devices * quota
    late_slots = n_cent * HALF
    depth = max(rows, n_samp * HALF)
    vmem = pl.BlockSpec(memory_space=pltpu.VMEM)
    anywhere = pl.BlockSpec(memory_space=pl.ANY)
    shape = jax.ShapeDtypeStruct
    dma = pltpu.SemaphoreType.DMA
    centroid, representative, back, meta = pl.pallas_call(
        functools.partial(
            dedup_kernel, n_samp, n_cent, groups, per_owner, quota, bin_rows, lane_rows
        ),
        out_shape=(
            shape((span, wide, LANES), BF),
            shape((span, wide, LANES), BF),
            shape((devices, 1, LANES), F32),
            shape((8, rows), I32),
        ),
        in_specs=[anywhere, vmem, vmem],
        out_specs=(vmem,) * 4,
        scratch_shapes=[
            pltpu.VMEM((rows, width), F32),
            pltpu.VMEM((depth, depth), BF),
            pltpu.VMEM((slots, width), BF),
            pltpu.VMEM((slots + late_slots, width), BF),
            pltpu.VMEM((devices, 1, LANES), F32),
            pltpu.VMEM((devices, 1, LANES), F32),
            pltpu.VMEM((n_samp, bin_rows, width), BF),
            pltpu.VMEM((n_samp, HALF, width), BF),
            pltpu.VMEM((n_samp, 1, LANES), F32),
            pltpu.VMEM((n_samp, 1, LANES), F32),
            pltpu.VMEM((n_cent, HALF, width), BF),
            pltpu.VMEM((n_cent, 1, LANES), F32),
            pltpu.VMEM((n_cent, 1, LANES), F32),
            pltpu.VMEM((slots + late_slots, LANES), F32),
            pltpu.VMEM((span * wide, LANES), F32),
            pltpu.VMEM((span, wide, LANES), BF),
            pltpu.VMEM((span, wide, LANES), BF),
            pltpu.VMEM((devices, 1, LANES), F32),
            dma((4,)), dma((4,)),
            dma((devices,)), dma((devices,)), dma((devices,)), dma((devices,)),
            dma((n_samp,)), dma((n_samp,)), dma((n_samp,)), dma((n_samp,)),
            dma((n_cent,)), dma((n_cent,)), dma((n_cent,)), dma((n_cent,)),
            dma((span,)), dma((span,)), dma((span,)), dma((span,)),
            dma((devices,)), dma((devices,)),
        ],
        compiler_params=pltpu.CompilerParams(collective_id=0, has_side_effects=True),
        name="dedup",
    )(embeddings, assignment.reshape(1, rows), owner_map.reshape(clusters // LANES, LANES))
    centroid, representative, keep, top = pl.pallas_call(
        functools.partial(finish_kernel, per_owner, n_cent),
        out_shape=(
            shape((per_owner, width), F32),
            shape((per_owner, width), F32),
            shape((1, rows), F32),
            shape((1, 1), F32),
        ),
        in_specs=[vmem] * 4,
        out_specs=(vmem, vmem, vmem, pl.BlockSpec(memory_space=pltpu.SMEM)),
        scratch_shapes=[pltpu.VMEM((span * wide, LANES), F32)],
        name="finish",
    )(centroid, representative, back, meta)
    keep = keep.reshape(rows)

    def fast(embeddings, assignment, owner_map, centroid, representative, keep):
        return centroid, representative, keep

    def slow(embeddings, assignment, owner_map, centroid, representative, keep):
        return full_capacity(embeddings, assignment, owner_map)

    spilled = top[0, 0] >= SPILL
    return lax.cond(
        spilled, slow, fast, embeddings, assignment, owner_map, centroid, representative, keep
    )


def solution(mesh):
    in_specs = (P(("samp", "cent"), None), P(("samp", "cent")), P())
    out_specs = (P(("samp", "cent"), None), P(("samp", "cent"), None), P(("samp", "cent")))
    return jax.shard_map(
        on_device, mesh=mesh, in_specs=in_specs, out_specs=out_specs, check_vma=False
    )
```

time: 59.1 us -> 58.5 us (0.990)
  Pallas kernels: 57.2 us -> 56.6 us
    pallas_call x1, Pallas kernels: 55.2 us -> 54.6 us  [on_device(): pl.pallas_call(functools.partial(dedup_kernel, n_samp, n_cent, groups, pe...]
where the time goes in v2:
time: 58.5 us; the launch traced here: 58.2 us
  Pallas kernels  56.6 us (97%)
  between operations  1.37 us (2%)
    pallas_call x1, Pallas kernels, on_device(): pl.pallas_call(functools.partial(dedup_kernel, n_samp, n_cent, groups, pe...  54.6 us
    pallas_call x1, Pallas kernels, on_device(): pl.pallas_call(functools.partial(finish_kernel, per_owner, n_cent), out_s...  2.06 us

profile of v2, /device:TPU:0, one launch (start us, length us, event | category | flops | bytes accessed | tf_op | source)
XLA Modules:
  0.0 58.2 jit_solution(14592556785138761713)
XLA Ops:
  0.6 54.6 %dedup.1 = (bf16[32,16,128]{2,1,0:T(8,128)(2,1)}, bf16[32,16,128]{2,1,0:T(8,128)(2,1)}, f32[32,1,128]{2,1,0:T(1,128)}, s32[8,512]{1,0:T(8,128)}) custom-call(f32[512,1024]{1,0:T(8,128)} %emb_hbm.1, s32[1,512]{1,0:T(1,128)} %bitcast.63, s32[16,128]{1,0:T(8,128)} %bitcast.52), custom_call_target="tpu_custom_call" | custom-call | tf_op jit(solution)/shard_map/dedup/pallas_call | solution.py:542
  55.2 2.1 %finish.1 = (f32[64,1024]{1,0:T(8,128)}, f32[64,1024]{1,0:T(8,128)}, f32[1,512]{1,0:T(1,128)}, f32[1,1]{1,0:T(1,128)}) custom-call(bf16[32,16,128]{2,1,0:T(8,128)(2,1)} %get-tuple-element.136.cent_ref, bf16[32,16,128]{2,1,0:T(8,128)(2,1)} %get-tuple-element.137.rep_ref, f32[32,1,128]{2,1,0:T(1,128)} %get-tuple-element.138.back_ref, ...), custom_call_target="tpu_custom_call" | custom-call | tf_op jit(solution)/shard_map/finish/pallas_call | solution.py:583
  57.8 0.2 conditional.1

commit v3 on v2

--- a/solution.py
+++ b/solution.py
@@ -49,8 +49,8 @@
 
 def dedup_kernel(
     n_samp, n_cent, groups, per_owner, quota, bin_rows, lane_rows,
-    emb_hbm, assign_ref, owner_ref, cent_ref, rep_ref, back_ref, meta_ref,
-    emb_ref, upper_ref, direct_ref, x_ref, tag_out_ref, tag_ref, bin_out_ref, bin_ref, note_out_ref, note_ref,
+    emb_hbm, assign_hbm, owner_hbm, cent_ref, rep_ref, back_ref, meta_hbm,
+    emb_ref, assign_ref, owner_ref, meta_ref, upper_ref, direct_ref, x_ref, tag_out_ref, tag_ref, bin_out_ref, bin_ref, note_out_ref, note_ref,
     lane_out_ref, mark_out_ref, mark_ref, col_ref, turn_ref, cent_out_ref, rep_out_ref, weight_ref,
     load_sem, own_sem, direct_out, direct_in, tag_out, tag_in, bin_out, bin_in, note_out, note_in,
     lane_out, lane_in, mark_out, mark_in, cent_send, cent_recv, rep_send, rep_recv, weight_out, weight_in,
@@ -83,12 +83,16 @@
             source, target, sent, received, device_id=device, device_id_type=MESH
         )
 
-    part = rows // load_sem.shape[0]
+    parts = load_sem.shape[0] - 2
+    part = rows // parts
     loads = [
+        pltpu.make_async_copy(assign_hbm, assign_ref, load_sem.at[parts]),
+        pltpu.make_async_copy(owner_hbm, owner_ref, load_sem.at[parts + 1]),
+    ] + [
         pltpu.make_async_copy(
             emb_hbm.at[pl.ds(i * part, part)], emb_ref.at[pl.ds(i * part, part)], load_sem.at[i]
         )
-        for i in range(load_sem.shape[0])
+        for i in range(parts)
     ]
     for copy in loads:
         copy.start()
@@ -103,6 +107,8 @@
         )
     upper_ref[...] = (iota(upper_ref.shape, 0) < iota(upper_ref.shape, 1)).astype(BF)
 
+    for copy in loads:
+        copy.wait()
     owner = owner_ref[...]
     owner_hot = (iota((table_rows, devices, LANES), 1) == owner[:, None, :]).astype(F32)
     before = dot(
@@ -145,8 +151,8 @@
         iota((8, rows), 0) == 0, dest, jnp.where(is_late, HALF + place, within)
     )
 
-    for copy in loads:
-        copy.wait()
+    keep_meta = pltpu.make_async_copy(meta_ref, meta_hbm, own_sem.at[4])
+    keep_meta.start()
     emb = emb_ref[...]
     unit = (emb * lax.rsqrt(jnp.sum(emb * emb, axis=1, keepdims=True) + EPSILON)).astype(BF)
     direct_seat = jnp.where(is_late, -1, dest * quota + within)
@@ -158,36 +164,51 @@
 
     def direct_copy(slot, device):
         at = pl.ds(slot * quota, quota)
-        return remote(direct_ref.at[at], x_ref.at[at], direct_out.at[slot], direct_in.at[slot], device)
+        return remote(direct_ref.at[at], x_ref.at[at], direct_out, direct_in, device)
 
     def tag_copy(slot, device):
-        return remote(tag_out_ref.at[slot], tag_ref.at[slot], tag_out.at[slot], tag_in.at[slot], device)
+        return remote(tag_out_ref.at[slot], tag_ref.at[slot], tag_out, tag_in, device)
 
     def bin_copy(a):
         return remote(
-            bin_out_ref.at[a], bin_ref.at[a, pl.ds(0, bin_rows)], bin_out.at[a], bin_in.at[a], (samps[a], cent)
+            bin_out_ref.at[a], bin_ref.at[a, pl.ds(0, bin_rows)], bin_out, bin_in, (samps[a], cent)
         )
 
     def note_copy(a):
-        return remote(note_out_ref.at[a], note_ref.at[a], note_out.at[a], note_in.at[a], (samps[a], cent))
+        return remote(note_out_ref.at[a], note_ref.at[a], note_out, note_in, (samps[a], cent))
 
     def lane_copy(b):
         return remote(
             lane_out_ref.at[b, pl.ds(0, lane_rows)], x_ref.at[pl.ds(slots + b * HALF, lane_rows)],
-            lane_out.at[b], lane_in.at[b], (samp, cents[b]),
+            lane_out, lane_in.at[b // 2], (samp, cents[b]),
         )
 
     def mark_copy(b):
-        return remote(mark_out_ref.at[b], mark_ref.at[b], mark_out.at[b], mark_in.at[b], (samp, cents[b]))
+        return remote(mark_out_ref.at[b], mark_ref.at[b], mark_out, mark_in, (samp, cents[b]))
 
     def cent_copy(slot, device):
-        return remote(cent_out_ref.at[slot], cent_ref.at[slot], cent_send.at[slot], cent_recv.at[slot], device)
+        return remote(cent_out_ref.at[slot], cent_ref.at[slot], cent_send, cent_recv, device)
 
     def rep_copy(slot, device):
-        return remote(rep_out_ref.at[slot], rep_ref.at[slot], rep_send.at[slot], rep_recv.at[slot], device)
+        return remote(rep_out_ref.at[slot], rep_ref.at[slot], rep_send, rep_recv, device)
 
     def weight_copy(slot, device):
-        return remote(weight_ref.at[slot], back_ref.at[slot], weight_out.at[slot], weight_in.at[slot], device)
+        return remote(weight_ref.at[slot], back_ref.at[slot], weight_out, weight_in, device)
+
+    def whole(ref, sent, received):
+        return remote(ref, ref, sent, received, (samps[1], cent))
+
+    all_direct = whole(direct_ref.at[pl.ds(0, slots - quota)], direct_out, direct_in)
+    all_tags = whole(tag_ref.at[pl.ds(0, devices - 1)], tag_out, tag_in)
+    all_bins = whole(bin_out_ref.at[pl.ds(0, n_samp - 1)], bin_out, bin_in)
+    all_notes = whole(note_ref.at[pl.ds(0, n_samp - 1)], note_out, note_in)
+    all_marks = whole(mark_ref.at[pl.ds(0, n_cent - 1)], mark_out, mark_in)
+    all_cents = whole(cent_out_ref.at[pl.ds(0, span - 1)], cent_send, cent_recv)
+    all_reps = whole(rep_out_ref.at[pl.ds(0, span - 1)], rep_send, rep_recv)
+    all_weights = whole(weight_ref.at[pl.ds(0, devices - 1)], weight_out, weight_in)
+
+    def some_lanes(b, count):
+        return whole(lane_out_ref.at[pl.ds(0, count), pl.ds(0, lane_rows)], lane_out, lane_in.at[b // 2])
 
     owners = [
         (a * near + b, (samps[a], cents[b]))
@@ -240,8 +261,7 @@
     for copy in local:
         copy.wait()
 
-    for a in range(1, n_samp):
-        note_copy(a).wait_recv()
+    all_notes.wait_recv()
     code = jnp.concatenate(
         [note_ref[j] + note_ref[j + 1] for j in range(0, n_samp, 2)], axis=1
     ).astype(I32)
@@ -264,8 +284,7 @@
         marks = row_dot(pieces, (iota((LANES, held), 0) == seat).astype(BF))
         mark_out_ref[b] = marks[0:1, :] + LANES * (marks[1:2, :] + HALF * marks[2:3, :])
     hot = (iota((late_slots, held), 0) == jnp.where(fits, to_cent * HALF + place, -1)).astype(BF)
-    for a in range(1, n_samp):
-        bin_copy(a).wait_recv()
+    all_bins.wait_recv()
     lane_out_ref[...] = (
         dot(hot, bin_ref[...].reshape(held, width)).astype(BF).reshape(n_cent, HALF, width)
     )
@@ -302,8 +321,7 @@
     def hit(tags):
         return (iota((per_owner, tags.shape[1]), 0) + 1).astype(F32) == tags
 
-    for slot, device in peers:
-        tag_copy(slot, device).wait_recv()
+    all_tags.wait_recv()
     tags = []
     for start in range(0, devices, pack):
         total = tag_ref[start]
@@ -312,14 +330,12 @@
         tags.append(total)
     tags = jnp.concatenate(tags, axis=1)
     columns(tags, 0)
-    for slot, device in peers:
-        direct_copy(slot, device).wait_recv()
+    all_direct.wait_recv()
     x = x_ref[0:slots, :]
     similar, density = score(0, slots, x, tags)
     sums = dot(hit(tags).astype(BF), x)
 
-    for b in range(1, n_cent):
-        mark_copy(b).wait_recv()
+    all_marks.wait_recv()
     sources = []
     columns_of = []
     for b in range(0, n_cent, 2):
@@ -333,9 +349,7 @@
         )
         at = slots + b * HALF
         columns(fresh_tags, at)
-        for c in (b, b + 1):
-            if c:
-                lane_copy(c).wait_recv()
+        some_lanes(b, 2 if b else 1).wait_recv()
         fresh = x_ref[at:at + LANES, :]
         sums = sums + dot(hit(fresh_tags).astype(BF), fresh)
         if b == n_cent - 2:
@@ -388,22 +402,14 @@
     for copy in local:
         copy.start()
 
-    for a in range(1, n_samp):
-        note_copy(a).wait_send()
-        bin_copy(a).wait_send()
-    for b in range(1, n_cent):
-        lane_copy(b).wait_send()
-        mark_copy(b).wait_send()
-    for slot, device in peers:
-        direct_copy(slot, device).wait_send()
-        tag_copy(slot, device).wait_send()
+    some_lanes(0, n_cent - 1).wait_send()
+    for copies in (all_notes, all_bins, all_marks, all_direct, all_tags):
+        copies.wait_send()
+    keep_meta.wait()
     for copy in local:
         copy.wait()
-    for slot, device in owners:
-        cent_copy(slot, device).wait()
-        rep_copy(slot, device).wait()
-    for slot, device in peers:
-        weight_copy(slot, device).wait()
+    for copies in (all_cents, all_reps, all_weights):
+        copies.wait()
 
 
 def finish_kernel(
@@ -549,10 +555,13 @@
             shape((devices, 1, LANES), F32),
             shape((8, rows), I32),
         ),
-        in_specs=[anywhere, vmem, vmem],
-        out_specs=(vmem,) * 4,
+        in_specs=[anywhere] * 3,
+        out_specs=(anywhere,) * 4,
         scratch_shapes=[
             pltpu.VMEM((rows, width), F32),
+            pltpu.VMEM((1, rows), I32),
+            pltpu.VMEM((clusters // LANES, LANES), I32),
+            pltpu.VMEM((8, rows), I32),
             pltpu.VMEM((depth, depth), BF),
             pltpu.VMEM((slots, width), BF),
             pltpu.VMEM((slots + late_slots, width), BF),
@@ -570,12 +579,9 @@
             pltpu.VMEM((span, wide, LANES), BF),
             pltpu.VMEM((span, wide, LANES), BF),
             pltpu.VMEM((devices, 1, LANES), F32),
-            dma((4,)), dma((4,)),
-            dma((devices,)), dma((devices,)), dma((devices,)), dma((devices,)),
-            dma((n_samp,)), dma((n_samp,)), dma((n_samp,)), dma((n_samp,)),
-            dma((n_cent,)), dma((n_cent,)), dma((n_cent,)), dma((n_cent,)),
-            dma((span,)), dma((span,)), dma((span,)), dma((span,)),
-            dma((devices,)), dma((devices,)),
+            dma((6,)), dma((5,)),
+            dma, dma, dma, dma, dma, dma, dma, dma,
+            dma, dma((n_cent // 2,)), dma, dma, dma, dma, dma, dma, dma, dma,
         ],
         compiler_params=pltpu.CompilerParams(collective_id=0, has_side_effects=True),
         name="dedup",

time: 58.5 us -> 53.7 us (0.918)
  Pallas kernels: 56.6 us -> 51.9 us
    pallas_call x1, Pallas kernels: 54.6 us -> 49.9 us  [on_device(): pl.pallas_call(functools.partial(dedup_kernel, n_samp, n_cent, groups, pe...]
where the time goes in v3:
time: 53.7 us; the launch traced here: 53.5 us
  Pallas kernels  51.9 us (97%)
  between operations  1.37 us (3%)
    pallas_call x1, Pallas kernels, on_device(): pl.pallas_call(functools.partial(dedup_kernel, n_samp, n_cent, groups, pe...  49.9 us
    pallas_call x1, Pallas kernels, on_device(): pl.pallas_call(functools.partial(finish_kernel, per_owner, n_cent), out_s...  2.06 us

profile of v3, /device:TPU:0, one launch (start us, length us, event | category | flops | bytes accessed | tf_op | source)
XLA Modules:
  0.0 53.5 jit_solution(6420391263260177482)
XLA Ops:
  0.6 49.9 %dedup.1 = (bf16[32,16,128]{2,1,0:T(8,128)(2,1)}, bf16[32,16,128]{2,1,0:T(8,128)(2,1)}, f32[32,1,128]{2,1,0:T(1,128)}, s32[8,512]{1,0:T(8,128)}) custom-call(f32[512,1024]{1,0:T(8,128)} %emb_hbm.1, s32[1,512]{1,0:T(1,128)} %bitcast.63, s32[16,128]{1,0:T(8,128)} %bitcast.52), custom_call_target="tpu_custom_call" | custom-call | tf_op jit(solution)/shard_map/dedup/pallas_call | solution.py:548
  50.5 2.1 %finish.1 = (f32[64,1024]{1,0:T(8,128)}, f32[64,1024]{1,0:T(8,128)}, f32[1,512]{1,0:T(1,128)}, f32[1,1]{1,0:T(1,128)}) custom-call(bf16[32,16,128]{2,1,0:T(8,128)(2,1)} %get-tuple-element.136.cent_ref, bf16[32,16,128]{2,1,0:T(8,128)(2,1)} %get-tuple-element.137.rep_ref, f32[32,1,128]{2,1,0:T(1,128)} %get-tuple-element.138.back_ref, ...), custom_call_target="tpu_custom_call" | custom-call | tf_op jit(solution)/shard_map/finish/pallas_call | solution.py:589
  53.1 0.2 conditional.1
